TPU v7x, 768 devices: a whole 4x8x12 slice. The times are simulated.
768 devices in a mesh: batch: 128 (over y, x, z_hi, core), tm: 6 (over z_lo).
Axes of the slice: x: 4, y: 8, z: 12 (z_hi: 2, z_lo: 6; z = z_hi * 6 + z_lo), core: 2. Of those that a mesh axis runs over, the one named last changes fastest.
Arguments:
- audio: bfloat16 [512, 768, 768], P('batch', 'tm'), as said below
- video: bfloat16 [512, 128, 1024], P('batch'), as said below
- pair_ids: int32 [512], P('batch'), may hold values from 0 to 511, each once
- windows: int32 [512], P('batch'), may hold values from 1 to 32, as said below
- lengths: int32 [512], P('batch'), may hold values from 192 to 768, as said below
- w_qkv: bfloat16 [768, 2304], replicated, as said below
- w_out: bfloat16 [768, 768], replicated, may hold values from -0.21875 to 0.21875
- w_query: bfloat16 [1024, 768], replicated, may hold values from -0.1875 to 0.1875
- w_audio_embed: bfloat16 [768, 768], replicated, may hold values from -0.21875 to 0.21875
- w_video_embed: bfloat16 [768, 768], replicated, may hold values from -0.21875 to 0.21875
Outputs:
- audio_mixed: bfloat16 [512, 768, 768], P('batch', 'tm')
- audio_embed: float32 [512, 768], P('batch')
- video_embed: float32 [512, 768], P('batch')
- logits: float32 [512, 512], P('batch')
- row_loss: float32 [512], P('batch')
Inputs may be any that keep to these rules, and one draw needn't show every extreme that they name: `pair_ids`: a permutation of the clip numbers. `windows`: some clip reaches 32 in every draw. `lengths`: some clip is valid over all 768 frames in every draw. `audio`: frame features. `video`: token features. `w_qkv`: projection weights of scale 768 to the minus one half.
All inputs are finite; a program needn't handle non-finite values.
Results may differ from a plain program's by a relative error of at most 0.0065.
Values may be sent and summed in bfloat16 or wider, within the bound.
A program may use at most 128 MiB of HBM per device.

v0:
```python
import jax
import jax.numpy as jnp
from jax import lax
from jax.sharding import PartitionSpec as P

HA = 12
HS = 64


NEG_LARGE = -1e30
LOGIT_SCALE = 10.0
LOGIT_BIAS = -10.0


def extended(block, sides, width):
    for axis, dim in sides:
        count = lax.axis_size(axis)
        forward = [(i, i + 1) for i in range(count - 1)]
        backward = [(target, source) for source, target in forward]
        low = lax.ppermute(
            lax.slice_in_dim(block, block.shape[dim] - width, None, axis=dim), axis, forward
        )
        high = lax.ppermute(lax.slice_in_dim(block, 0, width, axis=dim), axis, backward)
        block = jnp.concatenate([low, block, high], axis=dim)
    return block


def softmax_parts(scores, allowed):
    scores = jnp.where(allowed, scores, NEG_LARGE)
    highest = jnp.max(scores, axis=-1, keepdims=True)
    weights = jnp.where(allowed, jnp.exp(scores - highest), 0.0)
    return (highest, weights, jnp.sum(weights, axis=-1))


def unit_rows(matrix):
    return matrix / jnp.sqrt(jnp.sum(matrix * matrix, axis=1, keepdims=True) + 1e-06)


def per_device(
    audio, video, pair_ids, windows, lengths, w_qkv, w_out, w_query, w_audio_embed, w_video_embed
):
    clip_count, frame_count, model_width = audio.shape
    token_count = video.shape[1]
    tm_size = lax.axis_size("tm")
    tm_index = lax.axis_index("tm")
    local_width = model_width // tm_size
    local_heads = HA // tm_size
    total_frames = frame_count * tm_size
    halo_reach = frame_count // 4
    key_span = frame_count + 2 * halo_reach
    head_scale = HS ** (-0.5)
    flat_audio = audio.reshape(clip_count * frame_count, model_width)
    projected = jnp.dot(flat_audio, w_qkv, preferred_element_type=jnp.float32).astype(jnp.bfloat16)
    projected = projected.reshape(clip_count, frame_count, 3 * model_width)
    queries = projected[:, :, :model_width].reshape(clip_count, frame_count, HA, HS)
    key_value = projected[:, :, model_width:]
    padded = extended(key_value, (("tm", 1),), halo_reach)
    near_keys = padded[:, :, :model_width].reshape(clip_count, key_span, HA, HS)
    near_values = padded[:, :, model_width:].reshape(clip_count, key_span, HA, HS)
    query_pos = tm_index * frame_count + jnp.arange(frame_count, dtype=jnp.int32)
    key_pos = tm_index * frame_count - halo_reach + jnp.arange(key_span, dtype=jnp.int32)
    distance = jnp.abs(query_pos[:, None] - key_pos[None, :])
    inside = (key_pos >= 0) & (key_pos < total_frames)
    allowed = (distance[None] <= windows[:, None, None]) & inside[None, None, :]
    allowed = allowed & ((key_pos[None, None, :] < lengths[:, None, None]) | (distance == 0)[None])
    scores = (
        jnp.einsum("cqhd,ckhd->chqk", queries, near_keys, preferred_element_type=jnp.float32)
        * head_scale
    )
    highest, weights, totals = softmax_parts(scores, allowed[:, None])
    context = jnp.einsum(
        "chqk,ckhd->cqhd",
        weights.astype(jnp.bfloat16),
        near_values,
        preferred_element_type=jnp.float32,
    )
    context = context / jnp.transpose(totals, (0, 2, 1))[..., None]
    context = context.astype(jnp.bfloat16).reshape(clip_count * frame_count, model_width)
    mixed_rows = flat_audio.astype(jnp.float32) + jnp.dot(
        context, w_out, preferred_element_type=jnp.float32
    )
    audio_mixed = mixed_rows.astype(jnp.bfloat16).reshape(clip_count, frame_count, model_width)
    in_clip = query_pos[None, :] < lengths[:, None]
    frame_sum = jnp.sum(
        jnp.where(in_clip[:, :, None], audio_mixed.astype(jnp.float32), 0.0), axis=1
    )
    video_flat = video.reshape(clip_count * token_count, video.shape[2])
    query_cols = lax.dynamic_slice_in_dim(w_query, tm_index * local_width, local_width, 1)
    asking = jnp.dot(video_flat, query_cols, preferred_element_type=jnp.float32).astype(
        jnp.bfloat16
    )
    asking = asking.reshape(clip_count, token_count, local_heads, HS)
    far_keys, far_values = (
        lax.all_to_all(
            key_value[:, :, :model_width], "tm", split_axis=2, concat_axis=1, tiled=True
        ),
        lax.all_to_all(
            key_value[:, :, model_width:], "tm", split_axis=2, concat_axis=1, tiled=True
        ),
    )
    far_keys = far_keys.reshape(clip_count, total_frames, local_heads, HS)
    far_values = far_values.reshape(clip_count, total_frames, local_heads, HS)
    frame_valid = jnp.arange(total_frames, dtype=jnp.int32)[None, :] < lengths[:, None]
    cross_scores = (
        jnp.einsum("cqhd,ckhd->chqk", asking, far_keys, preferred_element_type=jnp.float32)
        * head_scale
    )
    cross_peak, cross_weights, cross_totals = softmax_parts(
        cross_scores, frame_valid[:, None, None, :]
    )
    heard_ctx = jnp.einsum(
        "chqk,ckhd->cqhd",
        cross_weights.astype(jnp.bfloat16),
        far_values,
        preferred_element_type=jnp.float32,
    )
    heard_ctx = heard_ctx / jnp.transpose(cross_totals, (0, 2, 1))[..., None]
    video_local = jnp.mean(heard_ctx, axis=1).reshape(clip_count, local_width).astype(jnp.bfloat16)
    embed_rows = lax.dynamic_slice_in_dim(w_video_embed, tm_index * local_width, local_width, 0)
    video_part = jnp.dot(video_local, embed_rows, preferred_element_type=jnp.float32)
    frame_sum, video_part = lax.psum((frame_sum, video_part), "tm")
    audio_pool = (frame_sum / lengths[:, None].astype(jnp.float32)).astype(jnp.bfloat16)
    audio_embed = unit_rows(jnp.dot(audio_pool, w_audio_embed, preferred_element_type=jnp.float32))
    video_embed = unit_rows(video_part)
    logits = (
        LOGIT_SCALE
        * jnp.dot(
            audio_embed,
            lax.all_gather(video_embed, "batch", axis=0, tiled=True).T,
            precision=lax.Precision.HIGHEST,
        )
        + LOGIT_BIAS
    )
    columns = jnp.arange(logits.shape[1], dtype=jnp.int32)
    pair_signs = jnp.where(columns[None, :] == pair_ids[:, None], 1.0, -1.0)
    row_loss = jnp.sum(jnp.logaddexp(0.0, -pair_signs * logits), axis=1)
    return (audio_mixed, audio_embed, video_embed, logits, row_loss)


def solution(mesh):
    in_specs = (
        P("batch", "tm", None),
        P("batch", None, None),
        P("batch"),
        P("batch"),
        P("batch"),
        P(),
        P(),
        P(),
        P(),
        P(),
    )
    out_specs = (
        P("batch", "tm", None),
        P("batch", None),
        P("batch", None),
        P("batch", None),
        P("batch"),
    )
    return jax.shard_map(
        per_device, mesh=mesh, in_specs=in_specs, out_specs=out_specs, check_vma=False
    )
```

profile of v0, /device:TPU:1, one launch (start us, length us, event | category | flops | bytes accessed | tf_op | source)
XLA Modules:
  0.0 293.2 jit_solution(14490013265499009398)
XLA Ops:
  7.2 2.0 copy-done
  9.2 3.1 %convolution_convert_fusion = bf16[512,2304]{1,0:T(8,128)(2,1)S(1)} fusion(bf16[512,768]{1,0:T(8,128)(2,1)} %bitcast.72, bf16[768,2304]{1,0:T(8,128)(2,1)S(1)} %copy-done), kind=kOutput, calls=%fused_computation.4 | convolution fusion | flops 1813118976 | bytes 6684672 | tf_op jit(solution)/shard_map/dot_general | solution.py:53
  14.5 2.2 copy.42
  16.7 12.8 %all-to-all-start.1 = ((bf16[4,128,768]{1,0,2:T(4,128)(2,1)}), bf16[4,128,768]{1,0,2:T(4,128)(2,1)}, u32[]{:S(2)}, u32[]{:S(2)}) async-start(bf16[4,128,768]{1,0,2:T(4,128)(2,1)} %copy.42), calls=%async_computation.1 | async-start | bytes 1572864 | tf_op jit(solution)/shard_map/all_to_all | solution.py:94
  29.4 2.1 fusion.54
  31.5 4.2 %collective-permute-start = (bf16[4,32,1536]{2,1,0:T(8,128)(2,1)}, bf16[4,32,1536]{2,1,0:T(8,128)(2,1)}, u32[]{:S(2)}, u32[]{:S(2)}) collective-permute-start(bf16[4,32,1536]{2,1,0:T(8,128)(2,1)} %get-tuple-element.12), channel_id=1, source_target_pairs={{0,1},{1,2},{2,3},{3,4},{4,5},{6,7},{7,8},{8,9},{9,10},{10,11},{12... | collective-permute-start | bytes 1179656 | tf_op jit(solution)/shard_map/ppermute | solution.py:20
  38.6 2.5 fusion.26
  41.7 2.7 slice.37
  45.9 2.2 copy.41
  48.1 2.3 copy.31
  52.1 5.6 %all-to-all-done.1 = bf16[4,128,768]{1,0,2:T(4,128)(2,1)} async-done(((bf16[4,128,768]{1,0,2:T(4,128)(2,1)}), bf16[4,128,768]{1,0,2:T(4,128)(2,1)}, u32[]{:S(2)}, u32[]{:S(2)}) %all-to-all-start.1) | async-done | bytes 786464 | tf_op jit(solution)/shard_map/all_to_all | solution.py:94
  57.8 5.0 %all-to-all-start = ((bf16[4,128,768]{1,0,2:T(4,128)(2,1)}), bf16[4,128,768]{1,0,2:T(4,128)(2,1)}, u32[]{:S(2)}, u32[]{:S(2)}) async-start(bf16[4,128,768]{1,0,2:T(4,128)(2,1)} %copy.41), calls=%async_computation | async-start | bytes 1572864 | tf_op jit(solution)/shard_map/all_to_all | solution.py:97
  66.2 2.5 copy.32
  68.7 2.5 copy.30
  71.2 6.0 %fusion.55 = (f32[4,12,128]{2,1,0:T(8,128)}, bf16[4,12,128,192]{2,3,1,0:T(8,128)(2,1)}) fusion(pred[4,128,192]{1,2,0:T(8,128)(4,1)} %or_and_fusion, bf16[4,128,12,64]{1,3,2,0:T(8,128)(2,1)} %bitcast.69, bf16[4,192,12,64]{1,3,2,0:T(8,128)(2,1)} %bitcast.66), kind=kOutput, calls=%fused_computation.72 | convolution fusion | flops 158073024 | bytes 4448256 | tf_op jit(solution)/shard_map/sub | solution.py:31
  77.2 3.2 %fusion.9 = bf16[4,128,12,64]{1,3,2,0:T(8,128)(2,1)S(1)} fusion(bf16[4,192,12,64]{1,3,2,0:T(8,128)(2,1)} %bitcast.67, bf16[4,12,128,192]{2,3,1,0:T(8,128)(2,1)} %get-tuple-element.15, f32[4,128,12]{1,2,0:T(8,128)} %bitcast.74), kind=kOutput, calls=%fused_computation.16 | convolution fusion | flops 151781376 | bytes 4349952 | tf_op jit(solution)/shard_map/chqk,ckhd->cqhd/dot_general | solution.py:71
  87.0 2.8 reshape.232
  93.9 2.8 reshape.229
  96.7 3.6 %fusion.56 = (f32[4,2,128]{2,1,0:T(2,128)S(1)}, bf16[4,2,128,768]{3,2,1,0:T(8,128)(2,1)}) fusion(pred[4,768]{1,0:T(4,128)(4,1)S(1)} %iota_compare_fusion, bf16[4,768,2,64]{1,3,2,0:T(8,128)(2,1)} %reshape.232, bf16[4,128,2,64]{1,0,3,2:T(4,128)(2,1)} %reshape.231), kind=kOutput, calls=%fused_computation.73 | convolution fusion | flops 105382656 | bytes 2497536 | tf_op jit(solution)/shard_map/sub | solution.py:31
  100.3 2.4 fusion.23
  104.5 31.3 %all-reduce = (f32[4,768]{1,0:T(4,128)}, f32[4,768]{1,0:T(4,128)S(1)}) all-reduce(f32[4,768]{1,0:T(4,128)} %select_reduce_fusion, f32[4,768]{1,0:T(4,128)} %fusion.35), channel_id=1, replica_groups=mesh['batch'=128,'tm'=6] {'tm'}, use_global_device_ids=true, to_apply=%region_3.4 | all-reduce | flops 6144 | bytes 49152 | tf_op jit(solution)/shard_map/psum | solution.py:121
  140.3 139.3 %all-gather.3.cloned.1.call-done = f32[128,4,768]{2,1,0:T(4,128)} async-done(((f32[1,4,768]{2,1,0:T(4,128)}), f32[128,4,768]{2,1,0:T(4,128)}) %all-gather.3.cloned.1.call-update) | async-done | bytes 1572880 | tf_op jit(solution)/shard_map/all_gather | solution.py:129
  279.6 2.7 reshape.234
  282.4 4.0 %select_reduce_fusion.1 = (f32[4]{0:T(128)}, f32[4,512]{1,0:T(4,128)}) fusion(s32[4]{0:T(128)S(1)} %copy-done.7, f32[4,768]{1,0:T(4,128)S(1)} %broadcast_divide_fusion.1, f32[512,768]{1,0:T(8,128)} %reshape.234), kind=kOutput, calls=%fused_computation.48 | convolution fusion | flops 18903036 | bytes 1593376 | tf_op jit(solution)/shard_map/dot_general | solution.py:127
  (58 shorter events, 29.3 us)
Async XLA Ops:
  7.2 2.0 copy-start
  12.3 2.2 copy-start.1
  16.7 20.4 %copy-start.4 = (s32[4]{0:T(128)S(1)}, s32[4]{0:T(128)}, u32[]{:S(2)}) copy-start(s32[4]{0:T(128)} %param.14) | copy-start | bytes 52
  16.7 41.1 %all-to-all-start.1 = ((bf16[4,128,768]{1,0,2:T(4,128)(2,1)}), bf16[4,128,768]{1,0,2:T(4,128)(2,1)}, u32[]{:S(2)}, u32[]{:S(2)}) async-start(bf16[4,128,768]{1,0,2:T(4,128)(2,1)} %copy.42), calls=%async_computation.1 | async-start | bytes 1572864 | tf_op jit(solution)/shard_map/all_to_all | solution.py:94
  31.5 31.3 %collective-permute-start = (bf16[4,32,1536]{2,1,0:T(8,128)(2,1)}, bf16[4,32,1536]{2,1,0:T(8,128)(2,1)}, u32[]{:S(2)}, u32[]{:S(2)}) collective-permute-start(bf16[4,32,1536]{2,1,0:T(8,128)(2,1)} %get-tuple-element.12), channel_id=1, source_target_pairs={{0,1},{1,2},{2,3},{3,4},{4,5},{6,7},{7,8},{8,9},{9,10},{10,11},{12... | collective-permute-start | bytes 1179656 | tf_op jit(solution)/shard_map/ppermute | solution.py:20
  35.7 27.1 %collective-permute-start.1 = (bf16[4,32,1536]{2,1,0:T(8,128)(2,1)}, bf16[4,32,1536]{2,1,0:T(8,128)(2,1)}, u32[]{:S(2)}, u32[]{:S(2)}) collective-permute-start(bf16[4,32,1536]{2,1,0:T(8,128)(2,1)} %get-tuple-element.13), channel_id=1, source_target_pairs={{1,0},{2,1},{3,2},{4,3},{5,4},{7,6},{8,7},{9,8},{10,9},{11,10},{13... | collective-permute-start | bytes 1179656 | tf_op jit(solution)/shard_map/ppermute | solution.py:23
  45.9 4.5 %copy-start.6 = (s32[4]{0:T(128)S(1)}, s32[4]{0:T(128)}, u32[]{:S(2)}) copy-start(s32[4]{0:T(128)} %param.13) | copy-start | bytes 52
  57.8 33.4 %all-to-all-start = ((bf16[4,128,768]{1,0,2:T(4,128)(2,1)}), bf16[4,128,768]{1,0,2:T(4,128)(2,1)}, u32[]{:S(2)}, u32[]{:S(2)}) async-start(bf16[4,128,768]{1,0,2:T(4,128)(2,1)} %copy.41), calls=%async_computation | async-start | bytes 1572864 | tf_op jit(solution)/shard_map/all_to_all | solution.py:97
  62.8 216.8 %all-gather.3.cloned.1.call-start = ((), (), s32[]{:S(2)}) async-start(), calls=%async_computation.2 | async-start | bytes 1585152 | tf_op jit(solution)/shard_map/all_gather | solution.py:129
  77.2 3.8 %copy-start.10 = (bf16[4,128,768]{2,1,0:T(8,128)(2,1)S(1)}, bf16[4,128,768]{2,1,0:T(8,128)(2,1)}, u32[]{:S(2)}) copy-start(bf16[4,128,768]{2,1,0:T(8,128)(2,1)} %param.10) | copy-start | bytes 2359300
  80.4 1.3 copy-start.9
  81.7 1.7 copy-start.8
  82.5 0.9 copy-start.2
  135.9 0.5 copy-start.5
  140.3 142.1 %copy-start.3 = (f32[4,768]{1,0:T(4,128)}, f32[4,768]{1,0:T(4,128)S(1)}, u32[]{:S(2)}) copy-start(f32[4,768]{1,0:T(4,128)S(1)} %broadcast_divide_fusion.1) | copy-start | bytes 36868
  140.3 142.1 %copy-start.7 = (s32[4]{0:T(128)S(1)}, s32[4]{0:T(128)}, u32[]{:S(2)}) copy-start(s32[4]{0:T(128)} %param.12) | copy-start | bytes 52
Sparse Core Ops, SparseCore 0:
  137.2 142.3 all-gather.2
where the time goes:
time: 294 us; the launch traced here: 293 us
  waiting for transfers between devices  146 us (50%)
  local copies, waits for them, and re-layouts  40.4 us (14%)
  blocking collectives  31.3 us (11%)
  matrix products  29 us (10%)
  starting transfers between devices  23.3 us (8%)
  between operations  14.2 us (5%)
  other arithmetic  8.73 us (3%)
    all_gather x1, waiting for transfers between devices, per_device(): lax.all_gather(video_embed, 'batch', axis=0, tiled=True)  139 us
    psum x1, blocking collectives, per_device(): frame_sum, video_part = lax.psum((frame_sum, video_part), 'tm')  31.3 us
    all_to_all x1, starting transfers between devices, per_device(): lax.all_to_all(key_value[:, :, :model_width], 'tm', split_axis=2, concat_...  12.8 us
    unnamed x25, local copies, waits for them, and re-layouts  11.8 us
    sub x2, matrix products, softmax_parts(): weights = jnp.where(allowed, jnp.exp(scores - highest), 0.0)  9.63 us
  transfers between devices with their start and end apart: 5, of which 3 were waited for; matrix products, arithmetic and copies ran while one was open for 16% of the time, Pallas kernels for 0%

commit v1 on v0

v1 whole, which is shorter than its diff:
```python
import jax
import jax.numpy as jnp
from jax import lax
from jax.experimental import pallas as pl
from jax.experimental.pallas import tpu as pltpu
from jax.sharding import PartitionSpec as P

NEG = -1e30
BF = jnp.bfloat16
F32 = jnp.float32
MESH = pl.DeviceIdType.MESH

CL = 4
FR = 128
D = 768
VT = 128
DV = 1024
PAIRS = 6
HALO = 32
EXT = FR + 2 * HALO
NX = 4
NZ = 2
NC = 2
NT = 6


def mm(a, b):
    return jnp.dot(a, b, preferred_element_type=F32)


def mmt(a, b):
    return lax.dot_general(a, b, (((1,), (1,)), ((), ())), preferred_element_type=F32)


def chunk(j, size):
    return pl.ds(pl.multiple_of(j * size, size), size)


def make_kernel(ny):
    clips_all = ny * NX * NZ * NC * CL

    def kernel(
        windows, lengths, pair_ids,
        audio_h, video_h, wqkv_h, wout_h, wask_h, wae_h, wve_h,
        mixed_o, ae_o, ve_o, logits_o, loss_o,
        audio_v, video_v, wq_v, wk_v, wv_v, wout_v, wask_v, wae_v, wve_v,
        hx, kx, vx, q_v, ask_v, o2_v, mt_v, lt_v, m_v, c_v, ctx_v, mixed_v,
        lse_all, fs_all, zp, gath, gp, ae_v, ve_v, lg_v,
        load_sem, out_sem, halo_s, halo_r, l_s, l_r, f_s, f_r, z_s, z_r,
        y_s, y_r, x_s, x_r, c_s, c_r,
    ):
        b = lax.axis_index("batch")
        t = lax.axis_index("tm")
        co = b % NC
        zh = (b // NC) % NZ
        x = (b // (NC * NZ)) % NX
        y = b // (NC * NZ * NX)
        z = zh * NT + t

        def batch_of(yy, xx, zz, cc):
            return ((yy * NX + xx) * NZ + zz) * NC + cc

        def load(src, dst, k):
            copy = pltpu.make_async_copy(src, dst, load_sem.at[k])
            copy.start()
            return copy

        ld_audio = load(audio_h, audio_v, 0)
        ld_k = load(wqkv_h.at[:, pl.ds(D, D)], wk_v, 1)
        ld_v = load(wqkv_h.at[:, pl.ds(2 * D, D)], wv_v, 2)
        ld_video = load(video_h, video_v, 3)
        ld_ask = load(wask_h, wask_v, 4)
        ld_q = load(wqkv_h.at[:, pl.ds(0, D)], wq_v, 5)
        ld_out = load(wout_h, wout_v, 6)
        ld_ve = load(wve_h, wve_v, 7)
        ld_ae = load(wae_h, wae_v, 8)

        def z_peer(k):
            zz = (z + k) % (NZ * NT)
            return (batch_of(y, x, zz // NT, co), zz % NT)

        def t_peer(k):
            return (b, (t + k) % NT)

        def y_peer(k):
            return (batch_of((y + k) % ny, x, zh, co), t)

        def x_peer(k):
            return (batch_of(y, (x + k) % NX, zh, co), t)

        core_peer = (batch_of(y, x, zh, 1 - co), t)

        peers = [z_peer(k) for k in range(1, NZ * NT)]
        peers += [y_peer(k) for k in range(1, ny)]
        peers += [x_peer(k) for k in range(1, NX)]
        peers += [core_peer]
        barrier = pltpu.get_barrier_semaphore()
        for peer in peers:
            pl.semaphore_signal(barrier, inc=1, device_id=peer, device_id_type=MESH)

        def remote(src, dst, s, r, peer):
            return pltpu.make_async_remote_copy(
                src_ref=src, dst_ref=dst, send_sem=s, recv_sem=r,
                device_id=peer, device_id_type=MESH,
            )

        ld_audio.wait()
        ld_k.wait()
        ld_v.wait()

        def kv_step(j, carry):
            cols = chunk(j, 256)
            rows = audio_v[...].reshape(CL * FR, D)
            kx[:, HALO:HALO + FR, cols] = mm(rows, wk_v[:, cols]).astype(BF).reshape(CL, FR, 256)
            vx[:, HALO:HALO + FR, cols] = mm(rows, wv_v[:, cols]).astype(BF).reshape(CL, FR, 256)
            return carry

        lax.fori_loop(0, 3, kv_step, 0)

        pl.semaphore_wait(barrier, len(peers))

        up = remote(
            audio_v.at[:, pl.ds(FR - HALO, HALO), :], hx.at[:, pl.ds(0, HALO), :],
            halo_s.at[0], halo_r.at[0], (b, jnp.minimum(t + 1, NT - 1)),
        )
        down = remote(
            audio_v.at[:, pl.ds(0, HALO), :], hx.at[:, pl.ds(HALO, HALO), :],
            halo_s.at[1], halo_r.at[1], (b, jnp.maximum(t - 1, 0)),
        )

        @pl.when(t < NT - 1)
        def _():
            up.start()

        @pl.when(t > 0)
        def _():
            down.start()

        @pl.when(t == 0)
        def _():
            hx[:, 0:HALO, :] = jnp.zeros((CL, HALO, D), BF)

        @pl.when(t == NT - 1)
        def _():
            hx[:, HALO:2 * HALO, :] = jnp.zeros((CL, HALO, D), BF)

        ld_video.wait()
        ld_ask.wait()

        def ask_step(j, carry):
            cols = chunk(j, 256)
            rows = video_v[...].reshape(CL * VT, DV)
            ask = mm(rows, wask_v[:, cols]).astype(BF) * jnp.asarray(0.125, BF)
            ask_v[:, :, cols] = ask.reshape(CL, VT, 256)
            return carry

        lax.fori_loop(0, 3, ask_step, 0)

        lane = lax.broadcasted_iota(jnp.int32, (128, 128), 1)
        low = lane < 64
        lane_row = lax.broadcasted_iota(jnp.int32, (1, 128), 1)
        ones = jnp.ones((128, 128), BF)
        zero_b = jnp.zeros((128, 128), BF)

        def cross_clip(c, carry):
            key_bias = jnp.where(t * FR + lane_row < lengths[c], 0.0, NEG)
            peak = jnp.zeros((128, 128), F32)
            total = jnp.zeros((128, 128), F32)
            for p in range(PAIRS):
                cols = slice(128 * p, 128 * p + 128)
                ask = ask_v[c, :, cols]
                ask2 = jnp.concatenate(
                    [jnp.where(low, ask, zero_b), jnp.where(low, zero_b, ask)], axis=0
                )
                keys = kx[c, HALO:HALO + FR, cols]
                values = vx[c, HALO:HALO + FR, cols]
                s = mmt(ask2, keys) + key_bias
                m = jnp.max(s, axis=1, keepdims=True)
                e = jnp.exp(s - m).astype(BF)
                o = mm(e, jnp.concatenate([values, ones], axis=1))
                for h in range(2):
                    rows = slice(128 * h, 128 * h + 128)
                    here = lane == (2 * p + h)
                    peak = jnp.where(here, m[rows], peak)
                    total = jnp.where(here, o[rows, 128:], total)
                    part = o[rows, :128].astype(BF)
                    o2_v[c * PAIRS + p, rows, :] = (
                        jnp.where(low, part, zero_b) if h == 0 else jnp.where(low, zero_b, part)
                    )
            mt_v[c] = peak
            lt_v[c] = total
            return carry

        lax.fori_loop(0, CL, cross_clip, 0)

        def table(ref):
            acc = ref[0]
            for c in range(1, CL):
                acc = acc + pltpu.roll(ref[c], 12 * c, 1)
            return jnp.transpose(acc)[0:48]

        peak48 = table(mt_v)
        m_v[...] = peak48
        lse_all[t] = peak48 + jnp.log(table(lt_v))

        l_copies = [
            remote(lse_all.at[t], lse_all.at[t], l_s.at[k], l_r.at[k], t_peer(k))
            for k in range(1, NT)
        ]
        for copy in l_copies:
            copy.start()

        ld_q.wait()

        def q_step(j, carry):
            cols = chunk(j, 256)
            rows = audio_v[...].reshape(CL * FR, D)
            q = mm(rows, wq_v[:, cols]).astype(BF) * jnp.asarray(0.125, BF)
            q_v[:, :, cols] = q.reshape(CL, FR, 256)
            return carry

        lax.fori_loop(0, 3, q_step, 0)

        @pl.when(t > 0)
        def _():
            up.wait_recv()

        @pl.when(t < NT - 1)
        def _():
            down.wait_recv()

        def halo_step(j, carry):
            cols = chunk(j, 256)
            rows = hx[...].reshape(CL * 2 * HALO, D)
            k = mm(rows, wk_v[:, cols]).astype(BF).reshape(CL, 2 * HALO, 256)
            kx[:, 0:HALO, cols] = k[:, :HALO]
            kx[:, HALO + FR:EXT, cols] = k[:, HALO:]
            v = mm(rows, wv_v[:, cols]).astype(BF).reshape(CL, 2 * HALO, 256)
            vx[:, 0:HALO, cols] = v[:, :HALO]
            vx[:, HALO + FR:EXT, cols] = v[:, HALO:]
            return carry

        lax.fori_loop(0, 3, halo_step, 0)
        ld_out.wait()

        row = lax.broadcasted_iota(jnp.int32, (128, 128), 0) % 64
        offset = row + HALO - lane
        distance = jnp.abs(offset)
        low64 = lane[:64] < 64
        zero_h = jnp.zeros((64, 128), BF)
        lane8 = lax.broadcasted_iota(jnp.int32, (8, 128), 1)

        def window_clip(c, carry):
            near = distance <= windows[c]
            length = lengths[c]
            for i in range(2):
                key_pos = lane + (t * FR + 64 * i - HALO)
                allowed = near & (key_pos >= 0) & ((key_pos < length) | (offset == 0))
                bias = jnp.where(allowed, 0.0, NEG)
                for p in range(PAIRS):
                    cols = slice(128 * p, 128 * p + 128)
                    q = q_v[c, 64 * i:64 * i + 64, cols]
                    q2 = jnp.concatenate(
                        [jnp.where(low64, q, zero_h), jnp.where(low64, zero_h, q)], axis=0
                    )
                    keys = kx[c, 64 * i:64 * i + 128, cols]
                    values = vx[c, 64 * i:64 * i + 128, cols]
                    s = mmt(q2, keys) + bias
                    m = jnp.max(s, axis=1, keepdims=True)
                    e = jnp.exp(s - m).astype(BF)
                    o = mm(e, jnp.concatenate([values, ones], axis=1))
                    top = jnp.where(low64, o[:64, :128], o[64:, :128])
                    bottom = jnp.where(low64, o[:64, 128:], o[64:, 128:])
                    ctx_v[64 * i:64 * i + 64, cols] = (top / bottom).astype(BF)
            in_clip = jnp.where(lane8 + t * FR < length, 1.0, 0.0).astype(BF)
            ctx = ctx_v[...]
            for j in range(3):
                cols = slice(256 * j, 256 * j + 256)
                mixed = mm(ctx, wout_v[:, cols]) + audio_v[c, :, cols].astype(F32)
                mixed = mixed.astype(BF)
                mixed_v[c, :, cols] = mixed
                fs_all[t, pl.ds(c, 1), cols] = mm(in_clip, mixed)[0:1]
            pltpu.make_async_copy(mixed_v.at[c], mixed_o.at[c], out_sem.at[c]).start()
            return carry

        lax.fori_loop(0, 2, window_clip, 0)

        for copy in l_copies:
            copy.wait()
        lse = lse_all[...]
        highest = jnp.max(lse, axis=0)
        whole = highest + jnp.log(jnp.sum(jnp.exp(lse - highest[None]), axis=0))
        c_v[...] = jnp.exp(m_v[...] - whole) * (1.0 / VT)
        for c in range(CL):
            for p in range(PAIRS):
                r = c * 12 + 2 * p
                pair = jnp.concatenate([c_v[r:r + 1], c_v[r + 1:r + 2]], axis=1).astype(BF)
                zp[z, c:c + 1, 128 * p:128 * p + 128] = mm(pair, o2_v[c * PAIRS + p])

        z_copies = [
            remote(zp.at[z], zp.at[z], z_s.at[k], z_r.at[k], z_peer(k))
            for k in range(1, NZ * NT)
        ]
        for copy in z_copies:
            copy.start()

        lax.fori_loop(2, CL, window_clip, 0)

        f_copies = [
            remote(fs_all.at[t], fs_all.at[t], f_s.at[k], f_r.at[k], t_peer(k))
            for k in range(1, NT)
        ]
        for copy in f_copies:
            copy.start()

        ld_ve.wait()
        for copy in z_copies:
            copy.wait()
        pools = jnp.concatenate(
            [jnp.sum(zp[0:NT], axis=0), jnp.sum(zp[NT:2 * NT], axis=0)], axis=0
        ).astype(BF)
        u = mm(pools, wve_v[...])
        embed = u / jnp.sqrt(jnp.sum(u * u, axis=1, keepdims=True) + 1e-06)
        gath[co, x, y] = embed.astype(BF)
        y_copies = [
            remote(gath.at[co, x, y], gath.at[co, x, y], y_s.at[k], y_r.at[k], y_peer(k))
            for k in range(1, ny)
        ]
        for copy in y_copies:
            copy.start()
        ve_v[...] = jnp.where(zh == 0, embed[:CL], embed[CL:])
        ve_out = pltpu.make_async_copy(ve_v, ve_o, out_sem.at[CL])
        ve_out.start()

        ld_ae.wait()
        for copy in f_copies:
            copy.wait()
        row4 = lax.broadcasted_iota(jnp.int32, (CL, 1), 0)
        count = jnp.zeros((CL, 1), F32)
        for c in range(CL):
            count = jnp.where(row4 == c, lengths[c].astype(F32), count)
        pool = jnp.sum(fs_all[...], axis=0) / count
        u = mm(jnp.concatenate([pool, pool], axis=0).astype(BF), wae_v[...])
        a_embed = u / jnp.sqrt(jnp.sum(u * u, axis=1, keepdims=True) + 1e-06)
        ae_v[...] = a_embed[:CL]
        ae_out = pltpu.make_async_copy(ae_v, ae_o, out_sem.at[CL + 1])
        ae_out.start()

        for copy in y_copies:
            copy.wait()
        x_copies = [
            remote(gath.at[co, x], gath.at[co, x], x_s.at[k], x_r.at[k], x_peer(k))
            for k in range(1, NX)
        ]
        for copy in x_copies:
            copy.start()
        c_copies = [
            remote(
                gath.at[co, (x + NX - k) % NX], gath.at[co, (x + NX - k) % NX],
                c_s.at[k], c_r.at[k], core_peer,
            )
            for k in range(NX)
        ]
        c_copies[0].start()
        for k in range(1, NX):
            x_copies[k - 1].wait()
            c_copies[k].start()
        for copy in c_copies:
            copy.wait()

        first = lax.broadcasted_iota(jnp.int32, (8, D), 0) < 4

        def order_rows(yy, carry):
            for xx in range(NX):
                one = gath[0, xx, yy].astype(F32)
                two = gath[1, xx, yy].astype(F32)
                top = jnp.where(first, one, pltpu.roll(two, 4, 0))
                bottom = jnp.where(first, pltpu.roll(one, 4, 0), two)
                gp[chunk(yy * NX + xx, 16), :] = jnp.concatenate([top, bottom], axis=0).astype(BF)
            return carry

        lax.fori_loop(0, ny, order_rows, 0)
        logits = mmt(a_embed.astype(BF), gp[...])[:CL] * 10.0 - 10.0
        lg_v[...] = logits
        lg_out = pltpu.make_async_copy(lg_v, logits_o, out_sem.at[CL + 2])
        lg_out.start()
        ids = jnp.zeros((CL, 1), jnp.int32)
        for c in range(CL):
            ids = jnp.where(row4 == c, pair_ids[c], ids)
        column = lax.broadcasted_iota(jnp.int32, (CL, clips_all), 1)
        signed = jnp.where(column == ids, -logits, logits)
        loss = jnp.maximum(signed, 0.0) + jnp.log1p(jnp.exp(-jnp.abs(signed)))
        for c in range(CL):
            loss_o[c] = jnp.sum(loss[c:c + 1])

        @pl.when(t < NT - 1)
        def _():
            up.wait_send()

        @pl.when(t > 0)
        def _():
            down.wait_send()

        for c in range(CL):
            pltpu.make_async_copy(mixed_v.at[c], mixed_o.at[c], out_sem.at[c]).wait()
        ve_out.wait()
        ae_out.wait()
        lg_out.wait()

    return kernel


def solution(mesh):
    nb = mesh.shape["batch"]
    ny = nb // (NX * NZ * NC)
    clips_all = nb * CL

    def per_device(
        audio, video, pair_ids, windows, lengths, w_qkv, w_out, w_query, w_audio_embed, w_video_embed
    ):
        smem = pl.BlockSpec(memory_space=pltpu.SMEM)
        hbm = pl.BlockSpec(memory_space=pl.ANY)
        dma = pltpu.SemaphoreType.DMA
        vm = pltpu.VMEM
        mixed, ae, ve, logits, loss = pl.pallas_call(
            make_kernel(ny),
            name="av_step",
            out_shape=(
                jax.ShapeDtypeStruct((CL, FR, D), BF),
                jax.ShapeDtypeStruct((CL, D), F32),
                jax.ShapeDtypeStruct((CL, D), F32),
                jax.ShapeDtypeStruct((CL, clips_all), F32),
                jax.ShapeDtypeStruct((CL,), F32),
            ),
            in_specs=[smem] * 3 + [hbm] * 7,
            out_specs=(hbm, hbm, hbm, hbm, smem),
            scratch_shapes=[
                vm((CL, FR, D), BF), vm((CL, VT, DV), BF),
                vm((D, D), BF), vm((D, D), BF), vm((D, D), BF), vm((D, D), BF),
                vm((DV, D), BF), vm((D, D), BF), vm((D, D), BF),
                vm((CL, 2 * HALO, D), BF), vm((CL, EXT, D), BF), vm((CL, EXT, D), BF),
                vm((CL, FR, D), BF), vm((CL, VT, D), BF), vm((CL * PAIRS, 256, 128), BF),
                vm((CL, 128, 128), F32), vm((CL, 128, 128), F32),
                vm((48, 128), F32), vm((48, 128), F32),
                vm((FR, D), BF), vm((CL, FR, D), BF),
                vm((NT, 48, 128), F32), vm((NT, CL, D), F32), vm((NZ * NT, CL, D), F32),
                vm((NC, NX, ny, 8, D), BF), vm((clips_all, D), BF),
                vm((CL, D), F32), vm((CL, D), F32), vm((CL, clips_all), F32),
                dma((9,)), dma((CL + 3,)), dma((2,)), dma((2,)),
                dma((NT,)), dma((NT,)), dma((NT,)), dma((NT,)),
                dma((NZ * NT,)), dma((NZ * NT,)),
                dma((ny,)), dma((ny,)), dma((NX,)), dma((NX,)), dma((NX,)), dma((NX,)),
            ],
            compiler_params=pltpu.CompilerParams(
                collective_id=0, has_side_effects=True, vmem_limit_bytes=56 * 1024 * 1024,
            ),
        )(windows, lengths, pair_ids, audio, video, w_qkv, w_out, w_query, w_audio_embed, w_video_embed)
        return mixed, ae, ve, logits, loss

    in_specs = (
        P("batch", "tm", None), P("batch", None, None), P("batch"), P("batch"), P("batch"),
        P(), P(), P(), P(), P(),
    )
    out_specs = (
        P("batch", "tm", None), P("batch", None), P("batch", None), P("batch", None), P("batch"),
    )
    return jax.shard_map(
        per_device, mesh=mesh, in_specs=in_specs, out_specs=out_specs, check_vma=False
    )
```

time: 294 us -> 65.3 us (0.22)
  waiting for transfers between devices: 146 us -> 0 us
  Pallas kernels: 0 us -> 60.1 us
  local copies, waits for them, and re-layouts: 40.4 us -> 4.4 us
  blocking collectives: 31.3 us -> 0 us
  matrix products: 29 us -> 0 us
  starting transfers between devices: 23.3 us -> 0 us
  between operations: 14.2 us -> 0.68 us
  other arithmetic: 8.73 us -> 0 us
    all_gather x1 -> x0, waiting for transfers between devices: 139 us -> none  [per_device(): lax.all_gather(video_embed, 'batch', axis=0, tiled=True)]
    pallas_call x0 -> x1, Pallas kernels: none -> 60.1 us  [per_device(): pl.pallas_call(make_kernel(ny), name='av_step', out_shape=(jax.ShapeDtype...]
    psum x1 -> x0, blocking collectives: 31.3 us -> none  [per_device(): frame_sum, video_part = lax.psum((frame_sum, video_part), 'tm')]
    dot_general x8 -> x0, matrix products: 19.4 us -> none  [the longest x1 4.02 us: per_device(): jnp.dot(audio_embed, lax.all_gather(video_embed, 'batch', axis=0, tiled=T...]
    all_to_all x2 -> x0, starting transfers between devices: 17.8 us -> none  [the longest x1 12.8 us: per_device(): lax.all_to_all(key_value[:, :, :model_width], 'tm', split_axis=2, concat_...]
    slice x7 -> x0, local copies, waits for them, and re-layouts: 15.2 us -> none  [the longest x2 4.09 us: per_device(): near_keys = padded[:, :, :model_width].reshape(clip_count, key_span, HA, HS)]
    sub x2 -> x0, matrix products: 9.63 us -> none  [softmax_parts(): weights = jnp.where(allowed, jnp.exp(scores - highest), 0.0)]
    unnamed x25 -> x13, local copies, waits for them, and re-layouts: 11.8 us -> 4.4 us
  transfers between devices with their start and end apart: 5 -> 0, of which waited for: 3 -> 0; matrix products, arithmetic and copies ran while one was open for 16% -> 0% of each run, Pallas kernels for 0% -> 0%
where the time goes in v1:
time: 65.3 us; the launch traced here: 65.2 us
  Pallas kernels  60.1 us (92%)
  local copies, waits for them, and re-layouts  4.4 us (7%)
  between operations  0.68 us (1%)
    pallas_call x1, Pallas kernels, per_device(): pl.pallas_call(make_kernel(ny), name='av_step', out_shape=(jax.ShapeDtype...  60.1 us
    unnamed x13, local copies, waits for them, and re-layouts  4.4 us

profile of v1, /device:TPU:1, one launch (start us, length us, event | category | flops | bytes accessed | tf_op | source)
XLA Modules:
  0.0 65.2 jit_solution(5533660408347376881)
XLA Ops:
  0.6 60.1 %av_step.1 = (bf16[4,128,768]{2,1,0:T(8,128)(2,1)}, f32[4,768]{1,0:T(4,128)}, f32[4,768]{1,0:T(4,128)}, f32[4,512]{1,0:T(4,128)}, f32[4]{0:T(128)}) custom-call(s32[4]{0:T(128)} %windows.1, s32[4]{0:T(128)} %lengths.1, s32[4]{0:T(128)} %pair_ids.1, bf16[4,128,768]{2,1,0:T(8,128)(2,1)} %audio_h.1, bf16[4,128,1024]{2,1,0:T(8,128)(2,1)} %video_h.1, ...), custom_call_target="tpu_custom_call" | custom-call | tf_op jit(solution)/shard_map/av_step/pallas_call | solution.py:425
  60.7 0.0 copy-start.1
  60.7 0.0 copy-start
  60.7 0.0 copy-start.2
  60.7 0.0 copy-start.3
  60.8 2.1 %copy.20 = bf16[4,128,768]{2,1,0:T(8,128)(2,1)} copy(bf16[4,128,768]{2,1,0:T(8,128)(2,1)} %get-tuple-element.10) | data formatting | bytes 1572864
  62.8 0.0 copy-done.1
  62.8 0.6 copy.21
  63.4 0.0 copy-done
  63.4 0.6 copy.22
  64.0 0.0 copy-done.2
  64.0 0.6 copy.23
  64.6 0.0 copy-done.3
  64.6 0.5 copy.24
Async XLA Ops:
  60.7 2.1 %copy-start.1 = (f32[4,768]{1,0:T(4,128)S(1)}, f32[4,768]{1,0:T(4,128)}, u32[]{:S(2)}) copy-start(f32[4,768]{1,0:T(4,128)} %get-tuple-element.11) | copy-start | bytes 36868
  60.7 2.7 %copy-start = (f32[4,768]{1,0:T(4,128)S(1)}, f32[4,768]{1,0:T(4,128)}, u32[]{:S(2)}) copy-start(f32[4,768]{1,0:T(4,128)} %get-tuple-element.12) | copy-start | bytes 36868
  60.7 3.3 %copy-start.2 = (f32[4,512]{1,0:T(4,128)S(1)}, f32[4,512]{1,0:T(4,128)}, u32[]{:S(2)}) copy-start(f32[4,512]{1,0:T(4,128)} %get-tuple-element.13) | copy-start | bytes 24580
  60.7 3.9 %copy-start.3 = (f32[4]{0:T(128)S(1)}, f32[4]{0:T(128)}, u32[]{:S(2)}) copy-start(f32[4]{0:T(128)} %get-tuple-element.14) | copy-start | bytes 52

commit v2 on v1

v2 whole, which is shorter than its diff:
```python
import jax
import jax.numpy as jnp
from jax import lax
from jax.experimental import pallas as pl
from jax.experimental.pallas import tpu as pltpu
from jax.sharding import PartitionSpec as P

NEG = -1e30
BF = jnp.bfloat16
F32 = jnp.float32
MESH = pl.DeviceIdType.MESH

CL = 4
FR = 128
D = 768
VT = 128
DV = 1024
PAIRS = 6
HALO = 32
EXT = FR + 2 * HALO
NX = 4
NZ = 2
NC = 2
NT = 6


def mm(a, b):
    return jnp.dot(a, b, preferred_element_type=F32)


def mmt(a, b):
    return lax.dot_general(a, b, (((1,), (1,)), ((), ())), preferred_element_type=F32)


def chunk(j, size):
    return pl.ds(pl.multiple_of(j * size, size), size)


def make_kernel(ny):
    clips_all = ny * NX * NZ * NC * CL

    def kernel(
        windows, lengths, pair_ids,
        audio_h, video_h, wqkv_h, wout_h, wask_h, wae_h, wve_h,
        mixed_o, ae_o, ve_o, logits_o, loss_o,
        audio_v, video_v, wq_v, wk_v, wv_v, wout_v, wask_v, wae_v, wve_v,
        hx, kx, vx, q_v, ask_v, e_v, o2_v, mt_v, lt_v, m_v, c_v, ctx_v, mixed_v,
        lse_all, fs_all, zp, gath, gp, ae_v, ve_v, lg_v,
        load_sem, out_sem, halo_s, halo_r, l_s, l_r, f_s, f_r, z_s, z_r,
        y_s, y_r, x_s, x_r, c_s, c_r,
    ):
        b = lax.axis_index("batch")
        t = lax.axis_index("tm")
        co = b % NC
        zh = (b // NC) % NZ
        x = (b // (NC * NZ)) % NX
        y = b // (NC * NZ * NX)
        z = zh * NT + t

        def batch_of(yy, xx, zz, cc):
            return ((yy * NX + xx) * NZ + zz) * NC + cc

        def load(src, dst, k):
            return pltpu.make_async_copy(src, dst, load_sem.at[k])

        ld_audio = load(audio_h, audio_v, 0)
        ld_k = load(wqkv_h.at[:, pl.ds(D, D)], wk_v, 1)
        ld_v = load(wqkv_h.at[:, pl.ds(2 * D, D)], wv_v, 2)
        ld_video = load(video_h, video_v, 3)
        ld_ask = load(wask_h, wask_v, 4)
        ld_q = load(wqkv_h.at[:, pl.ds(0, D)], wq_v, 5)
        ld_out = load(wout_h, wout_v, 6)
        ld_ve = load(wve_h, wve_v, 7)
        ld_ae = load(wae_h, wae_v, 8)
        ld_audio.start()
        ld_k.start()
        ld_video.start()
        ld_ask.start()
        def z_peer(k):
            zz = (z + k) % (NZ * NT)
            return (batch_of(y, x, zz // NT, co), zz % NT)

        def t_peer(k):
            return (b, (t + k) % NT)

        def y_peer(k):
            return (batch_of((y + k) % ny, x, zh, co), t)

        def x_peer(k):
            return (batch_of(y, (x + k) % NX, zh, co), t)

        core_peer = (batch_of(y, x, zh, 1 - co), t)

        peers = [z_peer(k) for k in range(1, NZ * NT)]
        peers += [y_peer(k) for k in range(1, ny)]
        peers += [x_peer(k) for k in range(1, NX)]
        peers += [core_peer]
        barrier = pltpu.get_barrier_semaphore()
        for peer in peers:
            pl.semaphore_signal(barrier, inc=1, device_id=peer, device_id_type=MESH)

        def remote(src, dst, s, r, peer):
            return pltpu.make_async_remote_copy(
                src_ref=src, dst_ref=dst, send_sem=s, recv_sem=r,
                device_id=peer, device_id_type=MESH,
            )

        def project(j, weight, dst):
            cols = chunk(j, 256)
            rows = audio_v[...].reshape(CL * FR, D)
            dst[:, HALO:HALO + FR, cols] = mm(rows, weight[:, cols]).astype(BF).reshape(CL, FR, 256)

        def k_step(j, carry):
            project(j, wk_v, kx)
            return carry

        def v_step(j, carry):
            project(j, wv_v, vx)
            return carry

        def q_step(j, carry):
            cols = chunk(j, 256)
            rows = audio_v[...].reshape(CL * FR, D)
            q = mm(rows, wq_v[:, cols]).astype(BF) * jnp.asarray(0.125, BF)
            q_v[:, :, cols] = q.reshape(CL, FR, 256)
            return carry

        def ask_step(j, carry):
            cols = chunk(j, 256)
            rows = video_v[...].reshape(CL * VT, DV)
            ask = mm(rows, wask_v[:, cols]).astype(BF) * jnp.asarray(0.125, BF)
            ask_v[:, :, cols] = ask.reshape(CL, VT, 256)
            return carry

        ld_audio.wait()
        ld_k.wait()
        ld_v.start()
        lax.fori_loop(0, 3, k_step, 0)
        ld_video.wait()
        ld_ask.wait()
        ld_q.start()
        ld_out.start()
        lax.fori_loop(0, 3, ask_step, 0)

        pl.semaphore_wait(barrier, len(peers))

        up = remote(
            audio_v.at[:, pl.ds(FR - HALO, HALO), :], hx.at[:, pl.ds(0, HALO), :],
            halo_s.at[0], halo_r.at[0], (b, jnp.minimum(t + 1, NT - 1)),
        )
        down = remote(
            audio_v.at[:, pl.ds(0, HALO), :], hx.at[:, pl.ds(HALO, HALO), :],
            halo_s.at[1], halo_r.at[1], (b, jnp.maximum(t - 1, 0)),
        )

        @pl.when(t < NT - 1)
        def _():
            up.start()

        @pl.when(t > 0)
        def _():
            down.start()

        @pl.when(t == 0)
        def _():
            hx[:, 0:HALO, :] = jnp.zeros((CL, HALO, D), BF)

        @pl.when(t == NT - 1)
        def _():
            hx[:, HALO:2 * HALO, :] = jnp.zeros((CL, HALO, D), BF)

        lane = lax.broadcasted_iota(jnp.int32, (128, 128), 1)
        low = lane < 64
        lane_row = lax.broadcasted_iota(jnp.int32, (1, 128), 1)
        ones = jnp.ones((128, 128), BF)
        zero_b = jnp.zeros((128, 128), BF)

        def split_heads(block):
            return jnp.concatenate(
                [jnp.where(low, block, zero_b), jnp.where(low, zero_b, block)], axis=0
            )

        def cross_clip(c, carry):
            key_bias = jnp.where(t * FR + lane_row < lengths[c], 0.0, NEG)
            peak = jnp.zeros((128, 128), F32)
            total = jnp.zeros((128, 128), F32)
            for p in range(PAIRS):
                cols = slice(128 * p, 128 * p + 128)
                s = mmt(ask_v[c, :, cols], split_heads(kx[c, HALO:HALO + FR, cols]))
                here = (lane & 63) == p
                tops, sums = [], []
                for h in range(2):
                    part = s[:, 128 * h:128 * h + 128] + key_bias
                    m = jnp.max(part, axis=1, keepdims=True)
                    e = jnp.exp(part - m)
                    tops.append(m)
                    sums.append(jnp.sum(e, axis=1, keepdims=True))
                    e_v[c * PAIRS + p, :, 128 * h:128 * h + 128] = e.astype(BF)
                peak = jnp.where(here, jnp.where(low, tops[0], tops[1]), peak)
                total = jnp.where(here, jnp.where(low, sums[0], sums[1]), total)
            mt_v[c] = peak
            lt_v[c] = total
            return carry

        lax.fori_loop(0, CL, cross_clip, 0)

        def table(ref):
            acc = ref[0]
            for c in range(1, CL):
                acc = acc + pltpu.roll(ref[c], PAIRS * c, 1)
            flat = jnp.transpose(acc)
            return jnp.concatenate([flat[0:24], flat[64:88]], axis=0)

        peak48 = table(mt_v)
        m_v[...] = peak48
        lse_all[t] = peak48 + jnp.log(table(lt_v))

        l_copies = [
            remote(lse_all.at[t], lse_all.at[t], l_s.at[k], l_r.at[k], t_peer(k))
            for k in range(1, NT)
        ]
        for copy in l_copies:
            copy.start()

        ld_v.wait()
        ld_ve.start()
        ld_ae.start()
        lax.fori_loop(0, 3, v_step, 0)

        def hear_clip(c, carry):
            for p in range(PAIRS):
                cols = slice(128 * p, 128 * p + 128)
                heard = mm(e_v[c * PAIRS + p], split_heads(vx[c, HALO:HALO + FR, cols]))
                o2_v[c * PAIRS + p] = heard.astype(BF)
            return carry

        lax.fori_loop(0, CL, hear_clip, 0)

        ld_q.wait()
        lax.fori_loop(0, 3, q_step, 0)

        @pl.when(t > 0)
        def _():
            up.wait_recv()

        @pl.when(t < NT - 1)
        def _():
            down.wait_recv()

        def halo_step(j, carry):
            cols = chunk(j, 256)
            rows = hx[...].reshape(CL * 2 * HALO, D)
            k = mm(rows, wk_v[:, cols]).astype(BF).reshape(CL, 2 * HALO, 256)
            kx[:, 0:HALO, cols] = k[:, :HALO]
            kx[:, HALO + FR:EXT, cols] = k[:, HALO:]
            v = mm(rows, wv_v[:, cols]).astype(BF).reshape(CL, 2 * HALO, 256)
            vx[:, 0:HALO, cols] = v[:, :HALO]
            vx[:, HALO + FR:EXT, cols] = v[:, HALO:]
            return carry

        lax.fori_loop(0, 3, halo_step, 0)

        for copy in l_copies:
            copy.wait()
        lse = lse_all[...]
        highest = jnp.max(lse, axis=0)
        whole = highest + jnp.log(jnp.sum(jnp.exp(lse - highest[None]), axis=0))
        c_v[...] = jnp.exp(m_v[...] - whole) * (1.0 / VT)
        for c in range(CL):
            for p in range(PAIRS):
                r = c * PAIRS + p
                pair = jnp.concatenate([c_v[r:r + 1], c_v[24 + r:25 + r]], axis=0).astype(BF)
                both = mm(pair, o2_v[r])
                zp[z, c:c + 1, 128 * p:128 * p + 128] = jnp.where(
                    lane_row < 64, both[0:1], both[1:2]
                )

        z_copies = [
            remote(zp.at[z], zp.at[z], z_s.at[k], z_r.at[k], z_peer(k))
            for k in range(1, NZ * NT)
        ]
        for copy in z_copies:
            copy.start()

        row64 = lax.broadcasted_iota(jnp.int32, (64, 128), 0)
        lane64 = lax.broadcasted_iota(jnp.int32, (64, 128), 1)
        offset = row64 + HALO - lane64
        distance = jnp.abs(offset)
        low64 = lane64 < 64

        def window_clip(c, carry):
            near = distance <= windows[c]
            length = lengths[c]
            for i in range(2):
                key_pos = lane64 + (t * FR + 64 * i - HALO)
                allowed = near & (key_pos >= 0) & ((key_pos < length) | (offset == 0))
                bias = jnp.where(allowed, 0.0, NEG)
                for p in range(PAIRS):
                    cols = slice(128 * p, 128 * p + 128)
                    keys = split_heads(kx[c, 64 * i:64 * i + 128, cols])
                    s = mmt(q_v[c, 64 * i:64 * i + 64, cols], keys)
                    es = []
                    for h in range(2):
                        part = s[:, 128 * h:128 * h + 128] + bias
                        m = jnp.max(part, axis=1, keepdims=True)
                        es.append(jnp.exp(part - m).astype(BF))
                    e = jnp.concatenate(es, axis=0)
                    values = vx[c, 64 * i:64 * i + 128, cols]
                    o = mm(e, jnp.concatenate([values, ones], axis=1))
                    top = jnp.where(low64, o[:64, :128], o[64:, :128])
                    bottom = jnp.where(low64, o[:64, 128:], o[64:, 128:])
                    ctx_v[c, 64 * i:64 * i + 64, cols] = (top / bottom).astype(BF)
            return carry

        lax.fori_loop(0, CL, window_clip, 0)

        ld_out.wait()
        frame = lax.broadcasted_iota(jnp.int32, (FR, 1), 0) + t * FR

        def out_step(j, carry):
            cols = chunk(j, 256)
            rows = ctx_v[...].reshape(CL * FR, D)
            mixed = mm(rows, wout_v[:, cols]).reshape(CL, FR, 256) + audio_v[:, :, cols].astype(F32)
            mixed = mixed.astype(BF)
            mixed_v[:, :, cols] = mixed
            wide = mixed.astype(F32)
            for c in range(CL):
                kept = jnp.where(frame < lengths[c], wide[c], 0.0)
                fs_all[t, c:c + 1, cols] = jnp.sum(kept, axis=0, keepdims=True)
            return carry

        lax.fori_loop(0, 3, out_step, 0)
        mixed_out = pltpu.make_async_copy(mixed_v, mixed_o, out_sem.at[0])
        mixed_out.start()

        f_copies = [
            remote(fs_all.at[t], fs_all.at[t], f_s.at[k], f_r.at[k], t_peer(k))
            for k in range(1, NT)
        ]
        for copy in f_copies:
            copy.start()

        ld_ve.wait()
        for copy in z_copies:
            copy.wait()
        pools = jnp.concatenate(
            [jnp.sum(zp[0:NT], axis=0), jnp.sum(zp[NT:2 * NT], axis=0)], axis=0
        ).astype(BF)
        u = mm(pools, wve_v[...])
        embed = u / jnp.sqrt(jnp.sum(u * u, axis=1, keepdims=True) + 1e-06)
        gath[co, x, y] = embed.astype(BF)
        around = [0]
        for k in range(1, ny // 2 + 1):
            around += [k] if 2 * k == ny else [k, ny - k]
        y_copies = {
            k: remote(gath.at[co, x, y], gath.at[co, x, y], y_s.at[k], y_r.at[k], y_peer(k))
            for k in around[1:]
        }

        step = 1 - 2 * co
        behind = (x + NX - step) % NX
        x_copies, c_copies = {}, []

        def to_core(k, n, xx):
            yy = (y + ny - k) % ny
            copy = remote(
                gath.at[co, xx, yy], gath.at[co, xx, yy],
                c_s.at[k, n], c_r.at[k, n], core_peer,
            )
            copy.start()
            c_copies.append(copy)

        def along_x(k):
            yy = (y + ny - k) % ny
            block = gath.at[co, x, yy]
            ahead = gath.at[co, behind, yy]
            x_copies[k] = [
                remote(block, block, x_s.at[k, 0], x_r.at[k, 0], x_peer(1)),
                remote(block, block, x_s.at[k, 1], x_r.at[k, 1], x_peer(NX - 1)),
                remote(ahead, ahead, x_s.at[k, 2], x_r.at[k, 2], (batch_of(y, (x + NX + step) % NX, zh, co), t)),
            ]
            x_copies[k][0].start()
            x_copies[k][1].start()
            to_core(k, 0, x)

        def pass_on(k):
            x_copies[k][0].wait_recv()
            x_copies[k][1].wait_recv()
            x_copies[k][2].start()
            to_core(k, 1, (x + NX - 1) % NX)
            to_core(k, 2, (x + 1) % NX)

        def last_x(k):
            x_copies[k][2].wait_recv()
            to_core(k, 3, (x + 2) % NX)

        for k in around[1:]:
            y_copies[k].start()
        along_x(0)
        ve_v[...] = jnp.where(zh == 0, embed[:CL], embed[CL:])
        ve_out = pltpu.make_async_copy(ve_v, ve_o, out_sem.at[1])
        ve_out.start()

        ld_ae.wait()
        for copy in f_copies:
            copy.wait()
        row4 = lax.broadcasted_iota(jnp.int32, (CL, 1), 0)
        count = jnp.zeros((CL, 1), F32)
        for c in range(CL):
            count = jnp.where(row4 == c, lengths[c].astype(F32), count)
        pool = jnp.sum(fs_all[...], axis=0) / count
        u = mm(jnp.concatenate([pool, pool], axis=0).astype(BF), wae_v[...])
        a_embed = u / jnp.sqrt(jnp.sum(u * u, axis=1, keepdims=True) + 1e-06)
        ae_v[...] = a_embed[:CL]
        ae_out = pltpu.make_async_copy(ae_v, ae_o, out_sem.at[2])
        ae_out.start()

        rounds = [around[0:1]] + [around[i:i + 2] for i in range(1, ny, 2)]
        for n in range(len(rounds) + 2):
            if 0 < n < len(rounds):
                for k in rounds[n]:
                    y_copies[k].wait_recv()
                    along_x(k)
            if 0 <= n - 1 < len(rounds):
                for k in rounds[n - 1]:
                    pass_on(k)
            if 0 <= n - 2 < len(rounds):
                for k in rounds[n - 2]:
                    last_x(k)
        for copy in c_copies:
            copy.wait()

        first = lax.broadcasted_iota(jnp.int32, (8, D), 0) < 4

        def order_rows(yy, carry):
            for xx in range(NX):
                one = gath[0, xx, yy].astype(F32)
                two = gath[1, xx, yy].astype(F32)
                top = jnp.where(first, one, pltpu.roll(two, 4, 0))
                bottom = jnp.where(first, pltpu.roll(one, 4, 0), two)
                gp[chunk(yy * NX + xx, 16), :] = jnp.concatenate([top, bottom], axis=0).astype(BF)
            return carry

        lax.fori_loop(0, ny, order_rows, 0)
        logits = mmt(a_embed.astype(BF), gp[...])[:CL] * 10.0 - 10.0
        lg_v[...] = logits
        lg_out = pltpu.make_async_copy(lg_v, logits_o, out_sem.at[3])
        lg_out.start()
        ids = jnp.zeros((CL, 1), jnp.int32)
        for c in range(CL):
            ids = jnp.where(row4 == c, pair_ids[c], ids)
        column = lax.broadcasted_iota(jnp.int32, (CL, clips_all), 1)
        signed = jnp.where(column == ids, -logits, logits)
        loss = jnp.maximum(signed, 0.0) + jnp.log1p(jnp.exp(-jnp.abs(signed)))
        for c in range(CL):
            loss_o[c] = jnp.sum(loss[c:c + 1])

        @pl.when(t < NT - 1)
        def _():
            up.wait_send()

        @pl.when(t > 0)
        def _():
            down.wait_send()

        for k in around[1:]:
            y_copies[k].wait_send()
        for k in around:
            for copy in x_copies[k]:
                copy.wait_send()
        mixed_out.wait()
        ve_out.wait()
        ae_out.wait()
        lg_out.wait()

    return kernel


def solution(mesh):
    nb = mesh.shape["batch"]
    ny = nb // (NX * NZ * NC)
    clips_all = nb * CL

    def per_device(
        audio, video, pair_ids, windows, lengths, w_qkv, w_out, w_query, w_audio_embed, w_video_embed
    ):
        smem = pl.BlockSpec(memory_space=pltpu.SMEM)
        hbm = pl.BlockSpec(memory_space=pl.ANY)
        dma = pltpu.SemaphoreType.DMA
        vm = pltpu.VMEM
        mixed, ae, ve, logits, loss = pl.pallas_call(
            make_kernel(ny),
            name="av_step",
            out_shape=(
                jax.ShapeDtypeStruct((CL, FR, D), BF),
                jax.ShapeDtypeStruct((CL, D), F32),
                jax.ShapeDtypeStruct((CL, D), F32),
                jax.ShapeDtypeStruct((CL, clips_all), F32),
                jax.ShapeDtypeStruct((CL,), F32),
            ),
            in_specs=[smem] * 3 + [hbm] * 7,
            out_specs=(hbm, hbm, hbm, hbm, smem),
            scratch_shapes=[
                vm((CL, FR, D), BF), vm((CL, VT, DV), BF),
                vm((D, D), BF), vm((D, D), BF), vm((D, D), BF), vm((D, D), BF),
                vm((DV, D), BF), vm((D, D), BF), vm((D, D), BF),
                vm((CL, 2 * HALO, D), BF), vm((CL, EXT, D), BF), vm((CL, EXT, D), BF),
                vm((CL, FR, D), BF), vm((CL, VT, D), BF), vm((CL * PAIRS, VT, 256), BF), vm((CL * PAIRS, VT, 128), BF),
                vm((CL, 128, 128), F32), vm((CL, 128, 128), F32),
                vm((48, 128), F32), vm((48, 128), F32),
                vm((CL, FR, D), BF), vm((CL, FR, D), BF),
                vm((NT, 48, 128), F32), vm((NT, CL, D), F32), vm((NZ * NT, CL, D), F32),
                vm((NC, NX, ny, 8, D), BF), vm((clips_all, D), BF),
                vm((CL, D), F32), vm((CL, D), F32), vm((CL, clips_all), F32),
                dma((9,)), dma((4,)), dma((2,)), dma((2,)),
                dma((NT,)), dma((NT,)), dma((NT,)), dma((NT,)),
                dma((NZ * NT,)), dma((NZ * NT,)),
                dma((ny,)), dma((ny,)), dma((ny, 3)), dma((ny, 3)), dma((ny, NX)), dma((ny, NX)),
            ],
            compiler_params=pltpu.CompilerParams(
                collective_id=0, has_side_effects=True, vmem_limit_bytes=56 * 1024 * 1024,
            ),
        )(windows, lengths, pair_ids, audio, video, w_qkv, w_out, w_query, w_audio_embed, w_video_embed)
        return mixed, ae, ve, logits, loss

    in_specs = (
        P("batch", "tm", None), P("batch", None, None), P("batch"), P("batch"), P("batch"),
        P(), P(), P(), P(), P(),
    )
    out_specs = (
        P("batch", "tm", None), P("batch", None), P("batch", None), P("batch", None), P("batch"),
    )
    return jax.shard_map(
        per_device, mesh=mesh, in_specs=in_specs, out_specs=out_specs, check_vma=False
    )
```

time: 65.3 us -> 71.4 us (1.093)
  Pallas kernels: 60.1 us -> 66.1 us
    pallas_call x1, Pallas kernels: 60.1 us -> 66.1 us  [per_device(): pl.pallas_call(make_kernel(ny), name='av_step', out_shape=(jax.ShapeDtype...]
where the time goes in v2:
time: 71.4 us; the launch traced here: 71.2 us
  Pallas kernels  66.1 us (93%)
  local copies, waits for them, and re-layouts  4.4 us (6%)
    pallas_call x1, Pallas kernels, per_device(): pl.pallas_call(make_kernel(ny), name='av_step', out_shape=(jax.ShapeDtype...  66.1 us
    unnamed x13, local copies, waits for them, and re-layouts  4.4 us

profile of v2, /device:TPU:1, one launch (start us, length us, event | category | flops | bytes accessed | tf_op | source)
XLA Modules:
  0.0 71.2 jit_solution(14577088466184764201)
XLA Ops:
  0.6 66.1 %av_step.1 = (bf16[4,128,768]{2,1,0:T(8,128)(2,1)}, f32[4,768]{1,0:T(4,128)}, f32[4,768]{1,0:T(4,128)}, f32[4,512]{1,0:T(4,128)}, f32[4]{0:T(128)}) custom-call(s32[4]{0:T(128)} %windows.1, s32[4]{0:T(128)} %lengths.1, s32[4]{0:T(128)} %pair_ids.1, bf16[4,128,768]{2,1,0:T(8,128)(2,1)} %audio_h.1, bf16[4,128,1024]{2,1,0:T(8,128)(2,1)} %video_h.1, ...), custom_call_target="tpu_custom_call" | custom-call | tf_op jit(solution)/shard_map/av_step/pallas_call | solution.py:491
  66.8 0.0 copy-start.1
  66.8 0.0 copy-start
  66.8 0.0 copy-start.2
  66.8 0.0 copy-start.3
  66.8 2.1 %copy.20 = bf16[4,128,768]{2,1,0:T(8,128)(2,1)} copy(bf16[4,128,768]{2,1,0:T(8,128)(2,1)} %get-tuple-element.10) | data formatting | bytes 1572864
  68.9 0.0 copy-done.1
  68.9 0.6 copy.21
  69.5 0.0 copy-done
  69.5 0.6 copy.22
  70.1 0.0 copy-done.2
  70.1 0.6 copy.23
  70.7 0.0 copy-done.3
  70.7 0.5 copy.24
Async XLA Ops:
  66.8 2.1 %copy-start.1 = (f32[4,768]{1,0:T(4,128)S(1)}, f32[4,768]{1,0:T(4,128)}, u32[]{:S(2)}) copy-start(f32[4,768]{1,0:T(4,128)} %get-tuple-element.11) | copy-start | bytes 36868
  66.8 2.7 %copy-start = (f32[4,768]{1,0:T(4,128)S(1)}, f32[4,768]{1,0:T(4,128)}, u32[]{:S(2)}) copy-start(f32[4,768]{1,0:T(4,128)} %get-tuple-element.12) | copy-start | bytes 36868
  66.8 3.3 %copy-start.2 = (f32[4,512]{1,0:T(4,128)S(1)}, f32[4,512]{1,0:T(4,128)}, u32[]{:S(2)}) copy-start(f32[4,512]{1,0:T(4,128)} %get-tuple-element.13) | copy-start | bytes 24580
  66.8 3.9 %copy-start.3 = (f32[4]{0:T(128)S(1)}, f32[4]{0:T(128)}, u32[]{:S(2)}) copy-start(f32[4]{0:T(128)} %get-tuple-element.14) | copy-start | bytes 52

commit v3 on v2

--- a/solution.py
+++ b/solution.py
@@ -36,17 +36,32 @@
     return pl.ds(pl.multiple_of(j * size, size), size)
 
 
+def write_out(mixed_v, ae_v, ve_v, lg_v, loss_v, mixed_o, ae_o, ve_o, lg_o, loss_o, sem):
+    copies = [
+        pltpu.make_async_copy(src, dst, sem.at[k])
+        for k, (src, dst) in enumerate(
+            ((mixed_v, mixed_o), (ae_v, ae_o), (ve_v, ve_o), (lg_v, lg_o))
+        )
+    ]
+    for copy in copies:
+        copy.start()
+    for c in range(CL):
+        loss_o[c] = jnp.max(loss_v[c:c + 1, :])
+    for copy in copies:
+        copy.wait()
+
+
 def make_kernel(ny):
     clips_all = ny * NX * NZ * NC * CL
 
     def kernel(
         windows, lengths, pair_ids,
         audio_h, video_h, wqkv_h, wout_h, wask_h, wae_h, wve_h,
-        mixed_o, ae_o, ve_o, logits_o, loss_o,
+        mixed_v, ae_v, ve_v, lg_v, loss_v,
         audio_v, video_v, wq_v, wk_v, wv_v, wout_v, wask_v, wae_v, wve_v,
-        hx, kx, vx, q_v, ask_v, e_v, o2_v, mt_v, lt_v, m_v, c_v, ctx_v, mixed_v,
-        lse_all, fs_all, zp, gath, gp, ae_v, ve_v, lg_v,
-        load_sem, out_sem, halo_s, halo_r, l_s, l_r, f_s, f_r, z_s, z_r,
+        hx, kx, vx, q_v, ask_v, e_v, o2_v, mt_v, lt_v, m_v, c_v, ctx_v,
+        lse_all, fs_all, share, zp, gath, gp,
+        load_sem, halo_s, halo_r, l_s, l_r, f_s, f_r, z_s, z_r,
         y_s, y_r, x_s, x_r, c_s, c_r,
     ):
         b = lax.axis_index("batch")
@@ -72,10 +87,8 @@
         ld_out = load(wout_h, wout_v, 6)
         ld_ve = load(wve_h, wve_v, 7)
         ld_ae = load(wae_h, wae_v, 8)
-        ld_audio.start()
-        ld_k.start()
-        ld_video.start()
-        ld_ask.start()
+        for copy in (ld_audio, ld_k, ld_video, ld_ask):
+            copy.start()
         def z_peer(k):
             zz = (z + k) % (NZ * NT)
             return (batch_of(y, x, zz // NT, co), zz % NT)
@@ -134,12 +147,11 @@
 
         ld_audio.wait()
         ld_k.wait()
-        ld_v.start()
         lax.fori_loop(0, 3, k_step, 0)
         ld_video.wait()
         ld_ask.wait()
-        ld_q.start()
-        ld_out.start()
+        for copy in (ld_v, ld_q, ld_ve, ld_out, ld_ae):
+            copy.start()
         lax.fori_loop(0, 3, ask_step, 0)
 
         pl.semaphore_wait(barrier, len(peers))
@@ -172,7 +184,6 @@
         lane = lax.broadcasted_iota(jnp.int32, (128, 128), 1)
         low = lane < 64
         lane_row = lax.broadcasted_iota(jnp.int32, (1, 128), 1)
-        ones = jnp.ones((128, 128), BF)
         zero_b = jnp.zeros((128, 128), BF)
 
         def split_heads(block):
@@ -180,24 +191,30 @@
                 [jnp.where(low, block, zero_b), jnp.where(low, zero_b, block)], axis=0
             )
 
+        marks = jnp.concatenate(
+            [jnp.where(low, 1.0, 0.0), jnp.where(low, 0.0, 1.0)], axis=0
+        ).astype(BF)
+
         def cross_clip(c, carry):
             key_bias = jnp.where(t * FR + lane_row < lengths[c], 0.0, NEG)
             peak = jnp.zeros((128, 128), F32)
             total = jnp.zeros((128, 128), F32)
+            pairs = [slice(128 * p, 128 * p + 128) for p in range(PAIRS)]
+            scores = [
+                mmt(ask_v[c, :, cols], split_heads(kx[c, HALO:HALO + FR, cols])) for cols in pairs
+            ]
             for p in range(PAIRS):
-                cols = slice(128 * p, 128 * p + 128)
-                s = mmt(ask_v[c, :, cols], split_heads(kx[c, HALO:HALO + FR, cols]))
                 here = (lane & 63) == p
-                tops, sums = [], []
+                tops, es = [], []
                 for h in range(2):
-                    part = s[:, 128 * h:128 * h + 128] + key_bias
+                    part = scores[p][:, 128 * h:128 * h + 128] + key_bias
                     m = jnp.max(part, axis=1, keepdims=True)
-                    e = jnp.exp(part - m)
                     tops.append(m)
-                    sums.append(jnp.sum(e, axis=1, keepdims=True))
-                    e_v[c * PAIRS + p, :, 128 * h:128 * h + 128] = e.astype(BF)
+                    es.append(jnp.exp(part - m).astype(BF))
+                e = jnp.concatenate(es, axis=1)
+                e_v[c * PAIRS + p] = e
                 peak = jnp.where(here, jnp.where(low, tops[0], tops[1]), peak)
-                total = jnp.where(here, jnp.where(low, sums[0], sums[1]), total)
+                total = jnp.where(here, mm(e, marks), total)
             mt_v[c] = peak
             lt_v[c] = total
             return carry
@@ -223,8 +240,6 @@
             copy.start()
 
         ld_v.wait()
-        ld_ve.start()
-        ld_ae.start()
         lax.fori_loop(0, 3, v_step, 0)
 
         def hear_clip(c, carry):
@@ -271,10 +286,11 @@
                 r = c * PAIRS + p
                 pair = jnp.concatenate([c_v[r:r + 1], c_v[24 + r:25 + r]], axis=0).astype(BF)
                 both = mm(pair, o2_v[r])
-                zp[z, c:c + 1, 128 * p:128 * p + 128] = jnp.where(
+                share[c:c + 1, 128 * p:128 * p + 128] = jnp.where(
                     lane_row < 64, both[0:1], both[1:2]
                 )
 
+        zp[z] = share[...].astype(BF)
         z_copies = [
             remote(zp.at[z], zp.at[z], z_s.at[k], z_r.at[k], z_peer(k))
             for k in range(1, NZ * NT)
@@ -286,30 +302,34 @@
         lane64 = lax.broadcasted_iota(jnp.int32, (64, 128), 1)
         offset = row64 + HALO - lane64
         distance = jnp.abs(offset)
-        low64 = lane64 < 64
 
         def window_clip(c, carry):
             near = distance <= windows[c]
             length = lengths[c]
+            biases = []
             for i in range(2):
                 key_pos = lane64 + (t * FR + 64 * i - HALO)
                 allowed = near & (key_pos >= 0) & ((key_pos < length) | (offset == 0))
-                bias = jnp.where(allowed, 0.0, NEG)
-                for p in range(PAIRS):
-                    cols = slice(128 * p, 128 * p + 128)
-                    keys = split_heads(kx[c, 64 * i:64 * i + 128, cols])
-                    s = mmt(q_v[c, 64 * i:64 * i + 64, cols], keys)
-                    es = []
-                    for h in range(2):
-                        part = s[:, 128 * h:128 * h + 128] + bias
-                        m = jnp.max(part, axis=1, keepdims=True)
-                        es.append(jnp.exp(part - m).astype(BF))
-                    e = jnp.concatenate(es, axis=0)
-                    values = vx[c, 64 * i:64 * i + 128, cols]
-                    o = mm(e, jnp.concatenate([values, ones], axis=1))
-                    top = jnp.where(low64, o[:64, :128], o[64:, :128])
-                    bottom = jnp.where(low64, o[:64, 128:], o[64:, 128:])
-                    ctx_v[c, 64 * i:64 * i + 64, cols] = (top / bottom).astype(BF)
+                biases.append(jnp.where(allowed, 0.0, NEG))
+            blocks = [
+                (i, slice(64 * i, 64 * i + 64), slice(64 * i, 64 * i + 128), slice(128 * p, 128 * p + 128))
+                for i in range(2) for p in range(PAIRS)
+            ]
+            scores = [
+                mmt(q_v[c, rows, cols], split_heads(kx[c, keys, cols])) for _, rows, keys, cols in blocks
+            ]
+            weights = []
+            for (i, _, _, _), s in zip(blocks, scores):
+                es = []
+                for h in range(2):
+                    part = s[:, 128 * h:128 * h + 128] + biases[i]
+                    m = jnp.max(part, axis=1, keepdims=True)
+                    es.append(jnp.exp(part - m).astype(BF))
+                weights.append(jnp.concatenate(es, axis=1))
+            for (_, rows, keys, cols), e in zip(blocks, weights):
+                values = split_heads(vx[c, keys, cols])
+                o = mm(e, jnp.concatenate([values, marks], axis=1))
+                ctx_v[c, rows, cols] = (o[:, :128] / o[:, 128:]).astype(BF)
             return carry
 
         lax.fori_loop(0, CL, window_clip, 0)
@@ -330,8 +350,6 @@
             return carry
 
         lax.fori_loop(0, 3, out_step, 0)
-        mixed_out = pltpu.make_async_copy(mixed_v, mixed_o, out_sem.at[0])
-        mixed_out.start()
 
         f_copies = [
             remote(fs_all.at[t], fs_all.at[t], f_s.at[k], f_r.at[k], t_peer(k))
@@ -344,7 +362,7 @@
         for copy in z_copies:
             copy.wait()
         pools = jnp.concatenate(
-            [jnp.sum(zp[0:NT], axis=0), jnp.sum(zp[NT:2 * NT], axis=0)], axis=0
+            [jnp.sum(zp[n:n + NT].astype(F32), axis=0) for n in (0, NT)], axis=0
         ).astype(BF)
         u = mm(pools, wve_v[...])
         embed = u / jnp.sqrt(jnp.sum(u * u, axis=1, keepdims=True) + 1e-06)
@@ -357,49 +375,9 @@
             for k in around[1:]
         }
 
-        step = 1 - 2 * co
-        behind = (x + NX - step) % NX
-        x_copies, c_copies = {}, []
-
-        def to_core(k, n, xx):
-            yy = (y + ny - k) % ny
-            copy = remote(
-                gath.at[co, xx, yy], gath.at[co, xx, yy],
-                c_s.at[k, n], c_r.at[k, n], core_peer,
-            )
-            copy.start()
-            c_copies.append(copy)
-
-        def along_x(k):
-            yy = (y + ny - k) % ny
-            block = gath.at[co, x, yy]
-            ahead = gath.at[co, behind, yy]
-            x_copies[k] = [
-                remote(block, block, x_s.at[k, 0], x_r.at[k, 0], x_peer(1)),
-                remote(block, block, x_s.at[k, 1], x_r.at[k, 1], x_peer(NX - 1)),
-                remote(ahead, ahead, x_s.at[k, 2], x_r.at[k, 2], (batch_of(y, (x + NX + step) % NX, zh, co), t)),
-            ]
-            x_copies[k][0].start()
-            x_copies[k][1].start()
-            to_core(k, 0, x)
-
-        def pass_on(k):
-            x_copies[k][0].wait_recv()
-            x_copies[k][1].wait_recv()
-            x_copies[k][2].start()
-            to_core(k, 1, (x + NX - 1) % NX)
-            to_core(k, 2, (x + 1) % NX)
-
-        def last_x(k):
-            x_copies[k][2].wait_recv()
-            to_core(k, 3, (x + 2) % NX)
-
         for k in around[1:]:
             y_copies[k].start()
-        along_x(0)
         ve_v[...] = jnp.where(zh == 0, embed[:CL], embed[CL:])
-        ve_out = pltpu.make_async_copy(ve_v, ve_o, out_sem.at[1])
-        ve_out.start()
 
         ld_ae.wait()
         for copy in f_copies:
@@ -412,48 +390,56 @@
         u = mm(jnp.concatenate([pool, pool], axis=0).astype(BF), wae_v[...])
         a_embed = u / jnp.sqrt(jnp.sum(u * u, axis=1, keepdims=True) + 1e-06)
         ae_v[...] = a_embed[:CL]
-        ae_out = pltpu.make_async_copy(ae_v, ae_o, out_sem.at[2])
-        ae_out.start()
-
-        rounds = [around[0:1]] + [around[i:i + 2] for i in range(1, ny, 2)]
-        for n in range(len(rounds) + 2):
-            if 0 < n < len(rounds):
-                for k in rounds[n]:
-                    y_copies[k].wait_recv()
-                    along_x(k)
-            if 0 <= n - 1 < len(rounds):
-                for k in rounds[n - 1]:
-                    pass_on(k)
-            if 0 <= n - 2 < len(rounds):
-                for k in rounds[n - 2]:
-                    last_x(k)
-        for copy in c_copies:
-            copy.wait()
-
+
+        for k in around[1:]:
+            y_copies[k].wait_recv()
+        step = 1 - 2 * co
+        behind = (x + NX - step) % NX
+
+        def to_core(n, xx):
+            copy = remote(gath.at[co, xx], gath.at[co, xx], c_s.at[n], c_r.at[n], core_peer)
+            copy.start()
+            return copy
+
+        block, ahead = gath.at[co, x], gath.at[co, behind]
+        x_copies = [
+            remote(block, block, x_s.at[0], x_r.at[0], x_peer(1)),
+            remote(block, block, x_s.at[1], x_r.at[1], x_peer(NX - 1)),
+            remote(ahead, ahead, x_s.at[2], x_r.at[2], (batch_of(y, (x + NX + step) % NX, zh, co), t)),
+        ]
+        x_copies[0].start()
+        x_copies[1].start()
+        c_copies = [to_core(0, x)]
+        x_copies[0].wait_recv()
+        x_copies[1].wait_recv()
+        x_copies[2].start()
+        c_copies.append(to_core(1, (x + NX - 1) % NX))
+        c_copies.append(to_core(2, (x + 1) % NX))
+        x_copies[2].wait_recv()
+        c_copies.append(to_core(3, (x + 2) % NX))
         first = lax.broadcasted_iota(jnp.int32, (8, D), 0) < 4
 
-        def order_rows(yy, carry):
-            for xx in range(NX):
+        for n, xx in enumerate((x, (x + NX - 1) % NX, (x + 1) % NX, (x + 2) % NX)):
+            c_copies[n].wait()
+
+            def order_rows(yy, carry, xx=xx):
                 one = gath[0, xx, yy].astype(F32)
                 two = gath[1, xx, yy].astype(F32)
                 top = jnp.where(first, one, pltpu.roll(two, 4, 0))
                 bottom = jnp.where(first, pltpu.roll(one, 4, 0), two)
                 gp[chunk(yy * NX + xx, 16), :] = jnp.concatenate([top, bottom], axis=0).astype(BF)
-            return carry
-
-        lax.fori_loop(0, ny, order_rows, 0)
+                return carry
+
+            lax.fori_loop(0, ny, order_rows, 0)
         logits = mmt(a_embed.astype(BF), gp[...])[:CL] * 10.0 - 10.0
         lg_v[...] = logits
-        lg_out = pltpu.make_async_copy(lg_v, logits_o, out_sem.at[3])
-        lg_out.start()
         ids = jnp.zeros((CL, 1), jnp.int32)
         for c in range(CL):
             ids = jnp.where(row4 == c, pair_ids[c], ids)
         column = lax.broadcasted_iota(jnp.int32, (CL, clips_all), 1)
         signed = jnp.where(column == ids, -logits, logits)
         loss = jnp.maximum(signed, 0.0) + jnp.log1p(jnp.exp(-jnp.abs(signed)))
-        for c in range(CL):
-            loss_o[c] = jnp.sum(loss[c:c + 1])
+        loss_v[...] = jnp.broadcast_to(jnp.sum(loss, axis=1, keepdims=True), (CL, 128))
 
         @pl.when(t < NT - 1)
         def _():
@@ -465,13 +451,8 @@
 
         for k in around[1:]:
             y_copies[k].wait_send()
-        for k in around:
-            for copy in x_copies[k]:
-                copy.wait_send()
-        mixed_out.wait()
-        ve_out.wait()
-        ae_out.wait()
-        lg_out.wait()
+        for copy in x_copies:
+            copy.wait_send()
 
     return kernel
 
@@ -488,18 +469,19 @@
         hbm = pl.BlockSpec(memory_space=pl.ANY)
         dma = pltpu.SemaphoreType.DMA
         vm = pltpu.VMEM
-        mixed, ae, ve, logits, loss = pl.pallas_call(
+        held = (
+            jax.ShapeDtypeStruct((CL, FR, D), BF),
+            jax.ShapeDtypeStruct((CL, D), F32),
+            jax.ShapeDtypeStruct((CL, D), F32),
+            jax.ShapeDtypeStruct((CL, clips_all), F32),
+            jax.ShapeDtypeStruct((CL, 128), F32),
+        )
+        parts = pl.pallas_call(
             make_kernel(ny),
             name="av_step",
-            out_shape=(
-                jax.ShapeDtypeStruct((CL, FR, D), BF),
-                jax.ShapeDtypeStruct((CL, D), F32),
-                jax.ShapeDtypeStruct((CL, D), F32),
-                jax.ShapeDtypeStruct((CL, clips_all), F32),
-                jax.ShapeDtypeStruct((CL,), F32),
-            ),
+            out_shape=tuple(vm(leaf.shape, leaf.dtype) for leaf in held),
             in_specs=[smem] * 3 + [hbm] * 7,
-            out_specs=(hbm, hbm, hbm, hbm, smem),
+            out_specs=(pl.BlockSpec(memory_space=vm),) * 5,
             scratch_shapes=[
                 vm((CL, FR, D), BF), vm((CL, VT, DV), BF),
                 vm((D, D), BF), vm((D, D), BF), vm((D, D), BF), vm((D, D), BF),
@@ -508,20 +490,27 @@
                 vm((CL, FR, D), BF), vm((CL, VT, D), BF), vm((CL * PAIRS, VT, 256), BF), vm((CL * PAIRS, VT, 128), BF),
                 vm((CL, 128, 128), F32), vm((CL, 128, 128), F32),
                 vm((48, 128), F32), vm((48, 128), F32),
-                vm((CL, FR, D), BF), vm((CL, FR, D), BF),
-                vm((NT, 48, 128), F32), vm((NT, CL, D), F32), vm((NZ * NT, CL, D), F32),
+                vm((CL, FR, D), BF),
+                vm((NT, 48, 128), F32), vm((NT, CL, D), F32), vm((CL, D), F32), vm((NZ * NT, CL, D), BF),
                 vm((NC, NX, ny, 8, D), BF), vm((clips_all, D), BF),
-                vm((CL, D), F32), vm((CL, D), F32), vm((CL, clips_all), F32),
-                dma((9,)), dma((4,)), dma((2,)), dma((2,)),
+                dma((9,)), dma((2,)), dma((2,)),
                 dma((NT,)), dma((NT,)), dma((NT,)), dma((NT,)),
                 dma((NZ * NT,)), dma((NZ * NT,)),
-                dma((ny,)), dma((ny,)), dma((ny, 3)), dma((ny, 3)), dma((ny, NX)), dma((ny, NX)),
+                dma((ny,)), dma((ny,)), dma((3,)), dma((3,)), dma((NX,)), dma((NX,)),
             ],
             compiler_params=pltpu.CompilerParams(
                 collective_id=0, has_side_effects=True, vmem_limit_bytes=56 * 1024 * 1024,
             ),
         )(windows, lengths, pair_ids, audio, video, w_qkv, w_out, w_query, w_audio_embed, w_video_embed)
-        return mixed, ae, ve, logits, loss
+        return pl.pallas_call(
+            write_out,
+            name="write_out",
+            out_shape=held[:4] + (jax.ShapeDtypeStruct((CL,), F32),),
+            in_specs=[pl.BlockSpec(memory_space=vm)] * 5,
+            out_specs=(hbm,) * 4 + (smem,),
+            scratch_shapes=[dma((4,))],
+            compiler_params=pltpu.CompilerParams(vmem_limit_bytes=4 * 1024 * 1024),
+        )(*parts)
 
     in_specs = (
         P("batch", "tm", None), P("batch", None, None), P("batch"), P("batch"), P("batch"),

time: 71.4 us -> 58.7 us (0.82)
  Pallas kernels: 66.1 us -> 57.9 us
  local copies, waits for them, and re-layouts: 4.4 us -> 0 us
    pallas_call x1 -> x2, Pallas kernels: 66.1 us -> 57.9 us  [the longest x1 56.4 us: per_device(): pl.pallas_call(make_kernel(ny), name='av_step', out_shape=tuple((vm(leaf....]
    unnamed x13 -> x0, local copies, waits for them, and re-layouts: 4.4 us -> none
where the time goes in v3:
time: 58.7 us; the launch traced here: 58.5 us
  Pallas kernels  57.9 us (99%)
  between operations  0.64 us (1%)
    pallas_call x1, Pallas kernels, per_device(): pl.pallas_call(make_kernel(ny), name='av_step', out_shape=tuple((vm(leaf....  56.4 us
    pallas_call x1, Pallas kernels, per_device(): pl.pallas_call(write_out, name='write_out', out_shape=held[:4] + (jax.Sha...  1.44 us

profile of v3, /device:TPU:1, one launch (start us, length us, event | category | flops | bytes accessed | tf_op | source)
XLA Modules:
  0.0 58.5 jit_solution(10698642223335431244)
XLA Ops:
  0.6 56.4 %av_step.1 = (bf16[4,128,768]{2,1,0:T(8,128)(2,1)S(1)}, f32[4,768]{1,0:T(4,128)S(1)}, f32[4,768]{1,0:T(4,128)S(1)}, f32[4,512]{1,0:T(4,128)S(1)}, f32[4,128]{1,0:T(4,128)S(1)}) custom-call(s32[4]{0:T(128)} %windows.1, s32[4]{0:T(128)} %lengths.1, s32[4]{0:T(128)} %pair_ids.1, bf16[4,128,768]{2,1,0:T(8,128)(2,1)} %audio_h.1, bf16[4,128,1024]{2,1,0:T(8,128)(2,1)} %video_h.1, ...), custom_call_target="tpu_custom_call" | custom-call | tf_op jit(solution)/shard_map/av_step/pallas_call | solution.py:479
  57.1 1.4 %write_out.1 = (bf16[4,128,768]{2,1,0:T(8,128)(2,1)}, f32[4,768]{1,0:T(4,128)}, f32[4,768]{1,0:T(4,128)}, f32[4,512]{1,0:T(4,128)}, f32[4]{0:T(128)}) custom-call(bf16[4,128,768]{2,1,0:T(8,128)(2,1)S(1)} %get-tuple-element.10.mixed_v, f32[4,768]{1,0:T(4,128)S(1)} %get-tuple-element.11.ae_v, f32[4,768]{1,0:T(4,128)S(1)} %get-tuple-element.12.ve_v, ...), custom_call_target="tpu_custom_call" | custom-call | tf_op jit(solution)/shard_map/write_out/pallas_call | solution.py:505

commit v4 on v3

--- a/solution.py
+++ b/solution.py
@@ -60,9 +60,9 @@
         mixed_v, ae_v, ve_v, lg_v, loss_v,
         audio_v, video_v, wq_v, wk_v, wv_v, wout_v, wask_v, wae_v, wve_v,
         hx, kx, vx, q_v, ask_v, e_v, o2_v, mt_v, lt_v, m_v, c_v, ctx_v,
-        lse_all, fs_all, share, zp, gath, gp,
+        lse_all, fs_all, share, zp, gath, gp, blocks, both_a, sums, other,
         load_sem, halo_s, halo_r, l_s, l_r, f_s, f_r, z_s, z_r,
-        y_s, y_r, x_s, x_r, c_s, c_r,
+        y_s, y_r, w_s, w_r, x_s, x_r, a_s, a_r, p_s, p_r,
     ):
         b = lax.axis_index("batch")
         t = lax.axis_index("tm")
@@ -104,10 +104,22 @@
 
         core_peer = (batch_of(y, x, zh, 1 - co), t)
 
+        def y_cross(k):
+            return (batch_of((y + k) % ny, x, zh, 1 - co), t)
+
+        def trio(k, other):
+            tt = (t // 3) * 3 + (t % 3 + k) % 3
+            return (batch_of(y, x, zh, 1 - co if other else co), tt)
+
+        far_y = sorted(range(1, ny), key=lambda k: -min(k, ny - k))
+        far_z = sorted(range(1, NZ * NT), key=lambda k: -min(k, NZ * NT - k))
+
         peers = [z_peer(k) for k in range(1, NZ * NT)]
         peers += [y_peer(k) for k in range(1, ny)]
         peers += [x_peer(k) for k in range(1, NX)]
         peers += [core_peer]
+        peers += [y_cross(k) for k in range(1, ny)]
+        peers += [trio(k, True) for k in (1, 2)]
         barrier = pltpu.get_barrier_semaphore()
         for peer in peers:
             pl.semaphore_signal(barrier, inc=1, device_id=peer, device_id_type=MESH)
@@ -153,33 +165,6 @@
         for copy in (ld_v, ld_q, ld_ve, ld_out, ld_ae):
             copy.start()
         lax.fori_loop(0, 3, ask_step, 0)
-
-        pl.semaphore_wait(barrier, len(peers))
-
-        up = remote(
-            audio_v.at[:, pl.ds(FR - HALO, HALO), :], hx.at[:, pl.ds(0, HALO), :],
-            halo_s.at[0], halo_r.at[0], (b, jnp.minimum(t + 1, NT - 1)),
-        )
-        down = remote(
-            audio_v.at[:, pl.ds(0, HALO), :], hx.at[:, pl.ds(HALO, HALO), :],
-            halo_s.at[1], halo_r.at[1], (b, jnp.maximum(t - 1, 0)),
-        )
-
-        @pl.when(t < NT - 1)
-        def _():
-            up.start()
-
-        @pl.when(t > 0)
-        def _():
-            down.start()
-
-        @pl.when(t == 0)
-        def _():
-            hx[:, 0:HALO, :] = jnp.zeros((CL, HALO, D), BF)
-
-        @pl.when(t == NT - 1)
-        def _():
-            hx[:, HALO:2 * HALO, :] = jnp.zeros((CL, HALO, D), BF)
 
         lane = lax.broadcasted_iota(jnp.int32, (128, 128), 1)
         low = lane < 64
@@ -232,12 +217,39 @@
         m_v[...] = peak48
         lse_all[t] = peak48 + jnp.log(table(lt_v))
 
+        pl.semaphore_wait(barrier, len(peers))
+
+        up = remote(
+            audio_v.at[:, pl.ds(FR - HALO, HALO), :], hx.at[:, pl.ds(0, HALO), :],
+            halo_s.at[0], halo_r.at[0], (b, jnp.minimum(t + 1, NT - 1)),
+        )
+        down = remote(
+            audio_v.at[:, pl.ds(0, HALO), :], hx.at[:, pl.ds(HALO, HALO), :],
+            halo_s.at[1], halo_r.at[1], (b, jnp.maximum(t - 1, 0)),
+        )
+
         l_copies = [
             remote(lse_all.at[t], lse_all.at[t], l_s.at[k], l_r.at[k], t_peer(k))
             for k in range(1, NT)
         ]
         for copy in l_copies:
             copy.start()
+
+        @pl.when(t < NT - 1)
+        def _():
+            up.start()
+
+        @pl.when(t > 0)
+        def _():
+            down.start()
+
+        @pl.when(t == 0)
+        def _():
+            hx[:, 0:HALO, :] = jnp.zeros((CL, HALO, D), BF)
+
+        @pl.when(t == NT - 1)
+        def _():
+            hx[:, HALO:2 * HALO, :] = jnp.zeros((CL, HALO, D), BF)
 
         ld_v.wait()
         lax.fori_loop(0, 3, v_step, 0)
@@ -253,27 +265,6 @@
 
         ld_q.wait()
         lax.fori_loop(0, 3, q_step, 0)
-
-        @pl.when(t > 0)
-        def _():
-            up.wait_recv()
-
-        @pl.when(t < NT - 1)
-        def _():
-            down.wait_recv()
-
-        def halo_step(j, carry):
-            cols = chunk(j, 256)
-            rows = hx[...].reshape(CL * 2 * HALO, D)
-            k = mm(rows, wk_v[:, cols]).astype(BF).reshape(CL, 2 * HALO, 256)
-            kx[:, 0:HALO, cols] = k[:, :HALO]
-            kx[:, HALO + FR:EXT, cols] = k[:, HALO:]
-            v = mm(rows, wv_v[:, cols]).astype(BF).reshape(CL, 2 * HALO, 256)
-            vx[:, 0:HALO, cols] = v[:, :HALO]
-            vx[:, HALO + FR:EXT, cols] = v[:, HALO:]
-            return carry
-
-        lax.fori_loop(0, 3, halo_step, 0)
 
         for copy in l_copies:
             copy.wait()
@@ -293,10 +284,31 @@
         zp[z] = share[...].astype(BF)
         z_copies = [
             remote(zp.at[z], zp.at[z], z_s.at[k], z_r.at[k], z_peer(k))
-            for k in range(1, NZ * NT)
+            for k in far_z
         ]
         for copy in z_copies:
             copy.start()
+
+        @pl.when(t > 0)
+        def _():
+            up.wait_recv()
+
+        @pl.when(t < NT - 1)
+        def _():
+            down.wait_recv()
+
+        def halo_step(j, carry):
+            cols = chunk(j, 256)
+            rows = hx[...].reshape(CL * 2 * HALO, D)
+            k = mm(rows, wk_v[:, cols]).astype(BF).reshape(CL, 2 * HALO, 256)
+            kx[:, 0:HALO, cols] = k[:, :HALO]
+            kx[:, HALO + FR:EXT, cols] = k[:, HALO:]
+            v = mm(rows, wv_v[:, cols]).astype(BF).reshape(CL, 2 * HALO, 256)
+            vx[:, 0:HALO, cols] = v[:, :HALO]
+            vx[:, HALO + FR:EXT, cols] = v[:, HALO:]
+            return carry
+
+        lax.fori_loop(0, 3, halo_step, 0)
 
         row64 = lax.broadcasted_iota(jnp.int32, (64, 128), 0)
         lane64 = lax.broadcasted_iota(jnp.int32, (64, 128), 1)
@@ -366,17 +378,21 @@
         ).astype(BF)
         u = mm(pools, wve_v[...])
         embed = u / jnp.sqrt(jnp.sum(u * u, axis=1, keepdims=True) + 1e-06)
-        gath[co, x, y] = embed.astype(BF)
-        around = [0]
-        for k in range(1, ny // 2 + 1):
-            around += [k] if 2 * k == ny else [k, ny - k]
-        y_copies = {
-            k: remote(gath.at[co, x, y], gath.at[co, x, y], y_s.at[k], y_r.at[k], y_peer(k))
-            for k in around[1:]
-        }
-
-        for k in around[1:]:
-            y_copies[k].start()
+        mine = (t % 3) * 2 + co
+        theirs = (t % 3) * 2 + 1 - co
+        for p in range(PAIRS):
+            blocks[p] = embed[:, 128 * p:128 * p + 128].astype(BF)
+        gath[x, y, co] = blocks[mine]
+        y_copies = [
+            remote(blocks.at[theirs], gath.at[x, y, co], w_s.at[k], w_r.at[k], y_cross(k))
+            for k in far_y + [0]
+        ]
+        y_copies += [
+            remote(blocks.at[mine], gath.at[x, y, co], y_s.at[k], y_r.at[k], y_peer(k))
+            for k in far_y
+        ]
+        for copy in y_copies:
+            copy.start()
         ve_v[...] = jnp.where(zh == 0, embed[:CL], embed[CL:])
 
         ld_ae.wait()
@@ -390,48 +406,54 @@
         u = mm(jnp.concatenate([pool, pool], axis=0).astype(BF), wae_v[...])
         a_embed = u / jnp.sqrt(jnp.sum(u * u, axis=1, keepdims=True) + 1e-06)
         ae_v[...] = a_embed[:CL]
-
-        for k in around[1:]:
-            y_copies[k].wait_recv()
-        step = 1 - 2 * co
-        behind = (x + NX - step) % NX
-
-        def to_core(n, xx):
-            copy = remote(gath.at[co, xx], gath.at[co, xx], c_s.at[n], c_r.at[n], core_peer)
-            copy.start()
-            return copy
-
-        block, ahead = gath.at[co, x], gath.at[co, behind]
+        both_a[co] = a_embed[:CL]
+        a_copy = remote(both_a.at[co], both_a.at[co], a_s, a_r, core_peer)
+        a_copy.start()
+
+        for copy in y_copies:
+            copy.wait()
         x_copies = [
-            remote(block, block, x_s.at[0], x_r.at[0], x_peer(1)),
-            remote(block, block, x_s.at[1], x_r.at[1], x_peer(NX - 1)),
-            remote(ahead, ahead, x_s.at[2], x_r.at[2], (batch_of(y, (x + NX + step) % NX, zh, co), t)),
-        ]
-        x_copies[0].start()
-        x_copies[1].start()
-        c_copies = [to_core(0, x)]
-        x_copies[0].wait_recv()
-        x_copies[1].wait_recv()
-        x_copies[2].start()
-        c_copies.append(to_core(1, (x + NX - 1) % NX))
-        c_copies.append(to_core(2, (x + 1) % NX))
-        x_copies[2].wait_recv()
-        c_copies.append(to_core(3, (x + 2) % NX))
-        first = lax.broadcasted_iota(jnp.int32, (8, D), 0) < 4
-
-        for n, xx in enumerate((x, (x + NX - 1) % NX, (x + 1) % NX, (x + 2) % NX)):
-            c_copies[n].wait()
-
-            def order_rows(yy, carry, xx=xx):
-                one = gath[0, xx, yy].astype(F32)
-                two = gath[1, xx, yy].astype(F32)
+            remote(gath.at[x], gath.at[x], x_s.at[k], x_r.at[k], x_peer(k)) for k in (2, 1, 3)
+        ]
+        for copy in x_copies:
+            copy.start()
+        first = lax.broadcasted_iota(jnp.int32, (8, 128), 0) < 4
+
+        def order(xx):
+            def order_rows(yy, carry):
+                one = gath[xx, yy, 0].astype(F32)
+                two = gath[xx, yy, 1].astype(F32)
                 top = jnp.where(first, one, pltpu.roll(two, 4, 0))
                 bottom = jnp.where(first, pltpu.roll(one, 4, 0), two)
                 gp[chunk(yy * NX + xx, 16), :] = jnp.concatenate([top, bottom], axis=0).astype(BF)
                 return carry
 
-            lax.fori_loop(0, ny, order_rows, 0)
-        logits = mmt(a_embed.astype(BF), gp[...])[:CL] * 10.0 - 10.0
+            lax.fori_loop(0, ny, order_rows, 0, unroll=True)
+
+        order(x)
+        a_copy.wait()
+        for copy in x_copies:
+            copy.wait()
+        for k in range(1, NX):
+            order((x + k) % NX)
+
+        cols = pl.ds(pl.multiple_of(mine * 128, 128), 128)
+        a8 = jnp.concatenate([both_a[0, :, cols], both_a[1, :, cols]], axis=0).astype(BF)
+        partial = mmt(a8, gp[...])
+        sums[mine] = jnp.where(co == 0, partial[:CL], partial[CL:])
+        other[...] = jnp.where(co == 0, partial[CL:], partial[:CL])
+        p_copies = [
+            remote(other, sums.at[mine], p_s.at[k], p_r.at[k], trio(k, True)) for k in range(3)
+        ]
+        p_copies += [
+            remote(sums.at[mine], sums.at[mine], p_s.at[2 + k], p_r.at[2 + k], trio(k, False))
+            for k in (1, 2)
+        ]
+        for copy in p_copies:
+            copy.start()
+        for copy in p_copies:
+            copy.wait()
+        logits = jnp.sum(sums[...], axis=0) * 10.0 - 10.0
         lg_v[...] = logits
         ids = jnp.zeros((CL, 1), jnp.int32)
         for c in range(CL):
@@ -448,11 +470,6 @@
         @pl.when(t > 0)
         def _():
             down.wait_send()
-
-        for k in around[1:]:
-            y_copies[k].wait_send()
-        for copy in x_copies:
-            copy.wait_send()
 
     return kernel
 
@@ -492,11 +509,13 @@
                 vm((48, 128), F32), vm((48, 128), F32),
                 vm((CL, FR, D), BF),
                 vm((NT, 48, 128), F32), vm((NT, CL, D), F32), vm((CL, D), F32), vm((NZ * NT, CL, D), BF),
-                vm((NC, NX, ny, 8, D), BF), vm((clips_all, D), BF),
+                vm((NX, ny, NC, 8, 128), BF), vm((clips_all, 128), BF),
+                vm((PAIRS, 8, 128), BF), vm((NC, CL, D), F32),
+                vm((6, CL, clips_all), F32), vm((CL, clips_all), F32),
                 dma((9,)), dma((2,)), dma((2,)),
                 dma((NT,)), dma((NT,)), dma((NT,)), dma((NT,)),
                 dma((NZ * NT,)), dma((NZ * NT,)),
-                dma((ny,)), dma((ny,)), dma((3,)), dma((3,)), dma((NX,)), dma((NX,)),
+                dma((ny,)), dma((ny,)), dma((ny,)), dma((ny,)), dma((NX,)), dma((NX,)), dma, dma, dma((5,)), dma((5,)),
             ],
             compiler_params=pltpu.CompilerParams(
                 collective_id=0, has_side_effects=True, vmem_limit_bytes=56 * 1024 * 1024,

time: 58.7 us -> 52.8 us (0.90)
  Pallas kernels: 57.9 us -> 52 us
    pallas_call x1, Pallas kernels: 56.4 us -> 50.6 us  [per_device(): pl.pallas_call(make_kernel(ny), name='av_step', out_shape=tuple((vm(leaf....]
where the time goes in v4:
time: 52.8 us; the launch traced here: 52.7 us
  Pallas kernels  52 us (98%)
  between operations  0.64 us (1%)
    pallas_call x1, Pallas kernels, per_device(): pl.pallas_call(make_kernel(ny), name='av_step', out_shape=tuple((vm(leaf....  50.6 us
    pallas_call x1, Pallas kernels, per_device(): pl.pallas_call(write_out, name='write_out', out_shape=held[:4] + (jax.Sha...  1.44 us

profile of v4, /device:TPU:1, one launch (start us, length us, event | category | flops | bytes accessed | tf_op | source)
XLA Modules:
  0.0 52.7 jit_solution(1720432695335504699)
XLA Ops:
  0.6 50.6 %av_step.1 = (bf16[4,128,768]{2,1,0:T(8,128)(2,1)S(1)}, f32[4,768]{1,0:T(4,128)S(1)}, f32[4,768]{1,0:T(4,128)S(1)}, f32[4,512]{1,0:T(4,128)S(1)}, f32[4,128]{1,0:T(4,128)S(1)}) custom-call(s32[4]{0:T(128)} %windows.1, s32[4]{0:T(128)} %lengths.1, s32[4]{0:T(128)} %pair_ids.1, bf16[4,128,768]{2,1,0:T(8,128)(2,1)} %audio_h.1, bf16[4,128,1024]{2,1,0:T(8,128)(2,1)} %video_h.1, ...), custom_call_target="tpu_custom_call" | custom-call | tf_op jit(solution)/shard_map/av_step/pallas_call | solution.py:496
  51.2 1.4 %write_out.1 = (bf16[4,128,768]{2,1,0:T(8,128)(2,1)}, f32[4,768]{1,0:T(4,128)}, f32[4,768]{1,0:T(4,128)}, f32[4,512]{1,0:T(4,128)}, f32[4]{0:T(128)}) custom-call(bf16[4,128,768]{2,1,0:T(8,128)(2,1)S(1)} %get-tuple-element.10.mixed_v, f32[4,768]{1,0:T(4,128)S(1)} %get-tuple-element.11.ae_v, f32[4,768]{1,0:T(4,128)S(1)} %get-tuple-element.12.ve_v, ...), custom_call_target="tpu_custom_call" | custom-call | tf_op jit(solution)/shard_map/write_out/pallas_call | solution.py:524

commit v5 on v4

--- a/solution.py
+++ b/solution.py
@@ -59,7 +59,7 @@
         audio_h, video_h, wqkv_h, wout_h, wask_h, wae_h, wve_h,
         mixed_v, ae_v, ve_v, lg_v, loss_v,
         audio_v, video_v, wq_v, wk_v, wv_v, wout_v, wask_v, wae_v, wve_v,
-        hx, kx, vx, q_v, ask_v, e_v, o2_v, mt_v, lt_v, m_v, c_v, ctx_v,
+        hx, kx, vx, q_v, ask_v, e_v, o2_v, mt_v, lt_v, m_v, ctx_v,
         lse_all, fs_all, share, zp, gath, gp, blocks, both_a, sums, other,
         load_sem, halo_s, halo_r, l_s, l_r, f_s, f_r, z_s, z_r,
         y_s, y_r, w_s, w_r, x_s, x_r, a_s, a_r, p_s, p_r,
@@ -188,18 +188,20 @@
             scores = [
                 mmt(ask_v[c, :, cols], split_heads(kx[c, HALO:HALO + FR, cols])) for cols in pairs
             ]
+            weights = []
             for p in range(PAIRS):
-                here = (lane & 63) == p
                 tops, es = [], []
                 for h in range(2):
                     part = scores[p][:, 128 * h:128 * h + 128] + key_bias
                     m = jnp.max(part, axis=1, keepdims=True)
                     tops.append(m)
                     es.append(jnp.exp(part - m).astype(BF))
-                e = jnp.concatenate(es, axis=1)
-                e_v[c * PAIRS + p] = e
-                peak = jnp.where(here, jnp.where(low, tops[0], tops[1]), peak)
-                total = jnp.where(here, mm(e, marks), total)
+                weights.append(jnp.concatenate(es, axis=1))
+                e_v[c * PAIRS + p] = weights[p]
+                peak = jnp.where((lane & 63) == p, jnp.where(low, tops[0], tops[1]), peak)
+            sums_all = mm(jnp.concatenate(weights, axis=0), marks)
+            for p in range(PAIRS):
+                total = jnp.where((lane & 63) == p, sums_all[VT * p:VT * p + VT], total)
             mt_v[c] = peak
             lt_v[c] = total
             return carry
@@ -235,22 +237,6 @@
         for copy in l_copies:
             copy.start()
 
-        @pl.when(t < NT - 1)
-        def _():
-            up.start()
-
-        @pl.when(t > 0)
-        def _():
-            down.start()
-
-        @pl.when(t == 0)
-        def _():
-            hx[:, 0:HALO, :] = jnp.zeros((CL, HALO, D), BF)
-
-        @pl.when(t == NT - 1)
-        def _():
-            hx[:, HALO:2 * HALO, :] = jnp.zeros((CL, HALO, D), BF)
-
         ld_v.wait()
         lax.fori_loop(0, 3, v_step, 0)
 
@@ -258,29 +244,42 @@
             for p in range(PAIRS):
                 cols = slice(128 * p, 128 * p + 128)
                 heard = mm(e_v[c * PAIRS + p], split_heads(vx[c, HALO:HALO + FR, cols]))
-                o2_v[c * PAIRS + p] = heard.astype(BF)
+                o2_v[c, :, cols] = heard.astype(BF)
             return carry
 
         lax.fori_loop(0, CL, hear_clip, 0)
 
         ld_q.wait()
         lax.fori_loop(0, 3, q_step, 0)
+
+        @pl.when(t < NT - 1)
+        def _():
+            up.start()
+
+        @pl.when(t > 0)
+        def _():
+            down.start()
+
+        @pl.when(t == 0)
+        def _():
+            hx[:, 0:HALO, :] = jnp.zeros((CL, HALO, D), BF)
+
+        @pl.when(t == NT - 1)
+        def _():
+            hx[:, HALO:2 * HALO, :] = jnp.zeros((CL, HALO, D), BF)
 
         for copy in l_copies:
             copy.wait()
         lse = lse_all[...]
         highest = jnp.max(lse, axis=0)
         whole = highest + jnp.log(jnp.sum(jnp.exp(lse - highest[None]), axis=0))
-        c_v[...] = jnp.exp(m_v[...] - whole) * (1.0 / VT)
+        parts = (jnp.exp(m_v[...] - whole) * (1.0 / VT)).astype(BF)
+        wide = lax.broadcasted_iota(jnp.int32, (48, D), 1)
+        source = ((wide >> 6) & 1) * 24 + (wide >> 7) - lax.broadcasted_iota(jnp.int32, (48, D), 0)
         for c in range(CL):
-            for p in range(PAIRS):
-                r = c * PAIRS + p
-                pair = jnp.concatenate([c_v[r:r + 1], c_v[24 + r:25 + r]], axis=0).astype(BF)
-                both = mm(pair, o2_v[r])
-                share[c:c + 1, 128 * p:128 * p + 128] = jnp.where(
-                    lane_row < 64, both[0:1], both[1:2]
-                )
-
+            heard = mm(parts, o2_v[c])
+            kept = jnp.where(source == -PAIRS * c, heard, 0.0)
+            share[c:c + 1, :] = jnp.sum(kept, axis=0, keepdims=True)
         zp[z] = share[...].astype(BF)
         z_copies = [
             remote(zp.at[z], zp.at[z], z_s.at[k], z_r.at[k], z_peer(k))
@@ -346,30 +345,6 @@
 
         lax.fori_loop(0, CL, window_clip, 0)
 
-        ld_out.wait()
-        frame = lax.broadcasted_iota(jnp.int32, (FR, 1), 0) + t * FR
-
-        def out_step(j, carry):
-            cols = chunk(j, 256)
-            rows = ctx_v[...].reshape(CL * FR, D)
-            mixed = mm(rows, wout_v[:, cols]).reshape(CL, FR, 256) + audio_v[:, :, cols].astype(F32)
-            mixed = mixed.astype(BF)
-            mixed_v[:, :, cols] = mixed
-            wide = mixed.astype(F32)
-            for c in range(CL):
-                kept = jnp.where(frame < lengths[c], wide[c], 0.0)
-                fs_all[t, c:c + 1, cols] = jnp.sum(kept, axis=0, keepdims=True)
-            return carry
-
-        lax.fori_loop(0, 3, out_step, 0)
-
-        f_copies = [
-            remote(fs_all.at[t], fs_all.at[t], f_s.at[k], f_r.at[k], t_peer(k))
-            for k in range(1, NT)
-        ]
-        for copy in f_copies:
-            copy.start()
-
         ld_ve.wait()
         for copy in z_copies:
             copy.wait()
@@ -395,6 +370,38 @@
             copy.start()
         ve_v[...] = jnp.where(zh == 0, embed[:CL], embed[CL:])
 
+        ld_out.wait()
+        frame = lax.broadcasted_iota(jnp.int32, (FR, 1), 0) + t * FR
+
+        def out_step(j, carry):
+            cols = chunk(j, 256)
+            rows = ctx_v[...].reshape(CL * FR, D)
+            mixed = mm(rows, wout_v[:, cols]).reshape(CL, FR, 256) + audio_v[:, :, cols].astype(F32)
+            mixed = mixed.astype(BF)
+            mixed_v[:, :, cols] = mixed
+            wide = mixed.astype(F32)
+            for c in range(CL):
+                kept = jnp.where(frame < lengths[c], wide[c], 0.0)
+                fs_all[t, c:c + 1, cols] = jnp.sum(kept, axis=0, keepdims=True)
+            return carry
+
+        lax.fori_loop(0, 3, out_step, 0)
+
+        f_copies = [
+            remote(fs_all.at[t], fs_all.at[t], f_s.at[k], f_r.at[k], t_peer(k))
+            for k in range(1, NT)
+        ]
+        for copy in f_copies:
+            copy.start()
+
+        for copy in y_copies:
+            copy.wait()
+        x_copies = [
+            remote(gath.at[x], gath.at[x], x_s.at[k], x_r.at[k], x_peer(k)) for k in (2, 1, 3)
+        ]
+        for copy in x_copies:
+            copy.start()
+
         ld_ae.wait()
         for copy in f_copies:
             copy.wait()
@@ -410,13 +417,6 @@
         a_copy = remote(both_a.at[co], both_a.at[co], a_s, a_r, core_peer)
         a_copy.start()
 
-        for copy in y_copies:
-            copy.wait()
-        x_copies = [
-            remote(gath.at[x], gath.at[x], x_s.at[k], x_r.at[k], x_peer(k)) for k in (2, 1, 3)
-        ]
-        for copy in x_copies:
-            copy.start()
         first = lax.broadcasted_iota(jnp.int32, (8, 128), 0) < 4
 
         def order(xx):
@@ -504,9 +504,9 @@
                 vm((D, D), BF), vm((D, D), BF), vm((D, D), BF), vm((D, D), BF),
                 vm((DV, D), BF), vm((D, D), BF), vm((D, D), BF),
                 vm((CL, 2 * HALO, D), BF), vm((CL, EXT, D), BF), vm((CL, EXT, D), BF),
-                vm((CL, FR, D), BF), vm((CL, VT, D), BF), vm((CL * PAIRS, VT, 256), BF), vm((CL * PAIRS, VT, 128), BF),
+                vm((CL, FR, D), BF), vm((CL, VT, D), BF), vm((CL * PAIRS, VT, 256), BF), vm((CL, VT, D), BF),
                 vm((CL, 128, 128), F32), vm((CL, 128, 128), F32),
-                vm((48, 128), F32), vm((48, 128), F32),
+                vm((48, 128), F32),
                 vm((CL, FR, D), BF),
                 vm((NT, 48, 128), F32), vm((NT, CL, D), F32), vm((CL, D), F32), vm((NZ * NT, CL, D), BF),
                 vm((NX, ny, NC, 8, 128), BF), vm((clips_all, 128), BF),

time: 52.8 us -> 52.9 us (level)
  no operation moved by 1% of the time
where the time goes in v5:
time: 52.9 us; the launch traced here: 52.8 us
  Pallas kernels  52.1 us (98%)
  between operations  0.64 us (1%)
    pallas_call x1, Pallas kernels, per_device(): pl.pallas_call(make_kernel(ny), name='av_step', out_shape=tuple((vm(leaf....  50.7 us
    pallas_call x1, Pallas kernels, per_device(): pl.pallas_call(write_out, name='write_out', out_shape=held[:4] + (jax.Sha...  1.44 us

profile of v5, /device:TPU:1, one launch (start us, length us, event | category | flops | bytes accessed | tf_op | source)
XLA Modules:
  0.0 52.8 jit_solution(5271849512513408452)
XLA Ops:
  0.6 50.7 %av_step.1 = (bf16[4,128,768]{2,1,0:T(8,128)(2,1)S(1)}, f32[4,768]{1,0:T(4,128)S(1)}, f32[4,768]{1,0:T(4,128)S(1)}, f32[4,512]{1,0:T(4,128)S(1)}, f32[4,128]{1,0:T(4,128)S(1)}) custom-call(s32[4]{0:T(128)} %windows.1, s32[4]{0:T(128)} %lengths.1, s32[4]{0:T(128)} %pair_ids.1, bf16[4,128,768]{2,1,0:T(8,128)(2,1)} %audio_h.1, bf16[4,128,1024]{2,1,0:T(8,128)(2,1)} %video_h.1, ...), custom_call_target="tpu_custom_call" | custom-call | tf_op jit(solution)/shard_map/av_step/pallas_call | solution.py:496
  51.3 1.4 %write_out.1 = (bf16[4,128,768]{2,1,0:T(8,128)(2,1)}, f32[4,768]{1,0:T(4,128)}, f32[4,768]{1,0:T(4,128)}, f32[4,512]{1,0:T(4,128)}, f32[4]{0:T(128)}) custom-call(bf16[4,128,768]{2,1,0:T(8,128)(2,1)S(1)} %get-tuple-element.10.mixed_v, f32[4,768]{1,0:T(4,128)S(1)} %get-tuple-element.11.ae_v, f32[4,768]{1,0:T(4,128)S(1)} %get-tuple-element.12.ve_v, ...), custom_call_target="tpu_custom_call" | custom-call | tf_op jit(solution)/shard_map/write_out/pallas_call | solution.py:524
